TPU v7x, 512 devices: a whole 4x8x8 slice. The times are simulated.
512 devices in a mesh: gx: 8 (over z), gy: 16 (over y, core), row: 4 (over x).
Axes of the slice: x: 4, y: 8, z: 8, core: 2. Of those that a mesh axis runs over, the one named last changes fastest.
Arguments:
- tokens: bfloat16 [4, 3584, 1664], P('row', 'gx', 'gy'), may hold values from -6 to 6
- segments: int32 [4, 3584], P('row'), may hold values from 0 to 31, never falling along the last dimension, each value on 1 to 2016 neighbouring positions
- gain_attn: float32 [1664], replicated, may hold values from 0.1 to 1.9
- w_query: bfloat16 [1664, 1664], P('gx', 'gy'), as said below
- w_key: bfloat16 [1664, 1664], P('gx', 'gy'), as said below
- w_value: bfloat16 [1664, 1664], P('gx', 'gy'), may hold values from -0.15625 to 0.15625
- w_out: bfloat16 [1664, 1664], P('gy'), may hold values from -0.15625 to 0.15625
- gain_mlp: float32 [1664], replicated, may hold values from 0.1 to 1.9
- w_up: bfloat16 [1664, 8192], P('gx', 'gy'), may hold values from -0.15625 to 0.15625
- w_down: bfloat16 [8192, 1664], P('gy', 'gx'), may hold values from -0.0625 to 0.0625
- w_merge: bfloat16 [4, 1664, 1664], P(None, 'gy', 'gx'), may hold values from -0.078125 to 0.078125
- merge_groups: int32 [4, 896, 4], P('row', 'gx'), may hold values from 0 to 447, as said below
- sources: int32 [4, 896], P('row', 'gx'), may hold values from 0 to 447, as said below
Outputs:
- layer_out: bfloat16 [4, 3584, 1664], P('row', 'gx', 'gy')
- returned: bfloat16 [4, 896, 1664], P('row', 'gx', 'gy')
Inputs may be any that keep to these rules, and one draw needn't show every extreme that they name: `segments`: ids never fall along a row group's tokens; each of the 32 ids holds 1 to 2016 tokens, one exactly 2016. `merge_groups`: for every row group and every block of 112 merged rows (one index of gx), the four positions of all its groups name each of 0 to 447 exactly once. `sources`: for every block b of 112 merged rows, the values over all row groups at that block name each of 0 to 447 exactly once. `w_query`: a real matrix whose entries lie within -161.2 and 161.2 over the square root of 1664. `w_key`: a real matrix whose entries lie within -4 and 4 over the square root of 1664.
All inputs are finite; a program needn't handle non-finite values.
Results may differ from a plain program's by a relative error of at most 0.029.
Values may be sent and summed in bfloat16 or wider, within the bound.
A program may use at most 64 MiB of HBM per device.

v0:
```python
import jax
import jax.numpy as jnp
from jax import lax
from jax.sharding import PartitionSpec as P

HD = 104


EPS = 1e-06
NEG = -1e30


def normalize(tok_rows, gain):
    tok_rows = tok_rows.astype(jnp.float32)
    row_mean = jnp.mean(tok_rows, axis=-1, keepdims=True)
    centred = tok_rows - row_mean
    row_var = jnp.mean(centred * centred, axis=-1, keepdims=True)
    return (centred * lax.rsqrt(row_var + EPS) * gain).astype(jnp.bfloat16)


def body(
    tokens,
    segments,
    gain_attn,
    w_query,
    w_key,
    w_value,
    w_out,
    gain_mlp,
    w_up,
    w_down,
    w_merge,
    merge_groups,
    sources,
):
    tok_local = tokens[0]
    row_count = tok_local.shape[0]
    seg_all = segments[0]
    col_count = w_query.shape[1]
    head_count = col_count // HD
    scale = HD ** (-0.5)
    gathered = lax.all_gather(tok_local, "gy", axis=1, tiled=True)
    normed = normalize(gathered, gain_attn)
    pieces = (
        lax.all_gather(w_query, "gx", axis=0, tiled=True),
        lax.all_gather(w_key, "gx", axis=0, tiled=True),
        lax.all_gather(w_value, "gx", axis=0, tiled=True),
    )
    feat_part = normed
    q_sum = jnp.dot(feat_part, pieces[0], preferred_element_type=jnp.float32)
    k_sum = jnp.dot(feat_part, pieces[1], preferred_element_type=jnp.float32)
    v_sum = jnp.dot(feat_part, pieces[2], preferred_element_type=jnp.float32)
    queries = q_sum.astype(jnp.bfloat16).reshape(row_count, head_count, HD)
    key_rows = k_sum.astype(jnp.bfloat16)
    value_rows = v_sum.astype(jnp.bfloat16)
    own_seg = lax.dynamic_slice_in_dim(seg_all, lax.axis_index("gx") * row_count, row_count)
    start_state = (
        jnp.full((row_count, head_count), NEG, jnp.float32),
        jnp.zeros((row_count, head_count), jnp.float32),
        jnp.zeros((row_count, head_count, HD), jnp.float32),
    )
    pieces = (
        lax.all_gather(key_rows, "gx", axis=0, tiled=True),
        lax.all_gather(value_rows, "gx", axis=0, tiled=True),
    )
    key_count = pieces[0].shape[0]
    block_len = min(row_count, key_count)
    block_total = key_count // block_len

    def one_block(step, old):
        block_keys = lax.dynamic_slice_in_dim(pieces[0], step * block_len, block_len, 0)
        block_values = lax.dynamic_slice_in_dim(pieces[1], step * block_len, block_len, 0)
        key_seg = lax.dynamic_slice_in_dim(seg_all, step * block_len, block_len)
        row_top, row_total, weighted = old
        key_heads = block_keys.reshape(block_len, head_count, HD)
        value_heads = block_values.reshape(block_len, head_count, HD)
        scores = (
            jnp.einsum("qhd,khd->qhk", queries, key_heads, preferred_element_type=jnp.float32)
            * scale
        )
        same_seg = (own_seg[:, None] == key_seg[None, :])[:, None, :]
        scores = jnp.where(same_seg, scores, NEG)
        new_top = jnp.maximum(row_top, jnp.max(scores, axis=-1))
        weights = jnp.where(same_seg, jnp.exp(scores - new_top[:, :, None]), 0.0)
        rescale = jnp.exp(row_top - new_top)
        row_total = row_total * rescale + jnp.sum(weights, axis=-1)
        weighted = weighted * rescale[:, :, None] + jnp.einsum(
            "qhk,khd->qhd",
            weights.astype(jnp.bfloat16),
            value_heads,
            preferred_element_type=jnp.float32,
        )
        return (new_top, row_total, weighted)

    row_top, row_total, weighted = lax.fori_loop(0, block_total, one_block, start_state)
    attended = (weighted / row_total[:, :, None]).reshape(row_count, col_count).astype(jnp.bfloat16)
    out_cols = lax.all_to_all(w_out, "gy", split_axis=1, concat_axis=0, tiled=True)
    attn_out = jnp.dot(
        lax.all_gather(attended, "gy", axis=1, tiled=True),
        out_cols,
        preferred_element_type=jnp.float32,
    )
    after_attn = (tok_local.astype(jnp.float32) + attn_out).astype(jnp.bfloat16)
    gathered_mlp = lax.all_gather(after_attn, "gy", axis=1, tiled=True)
    normed_mlp = normalize(gathered_mlp, gain_mlp)
    feat_part = normed_mlp
    hidden_sum = jnp.dot(
        feat_part,
        lax.all_gather(w_up, "gx", axis=0, tiled=True),
        preferred_element_type=jnp.float32,
    )
    hidden = jax.nn.gelu(hidden_sum, approximate=False).astype(jnp.bfloat16)
    partials = jnp.dot(
        hidden, lax.all_gather(w_down, "gx", axis=1, tiled=True), preferred_element_type=jnp.float32
    )
    mlp_out = lax.psum_scatter(
        partials.astype(jnp.bfloat16), "gy", scatter_dimension=1, tiled=True
    ).astype(jnp.float32)
    after_mlp = (after_attn.astype(jnp.float32) + mlp_out).astype(jnp.bfloat16)
    picked = after_mlp[merge_groups[0]]
    merge_terms = jnp.einsum(
        "mkc,kcn->mn",
        picked,
        lax.all_gather(w_merge, "gx", axis=2, tiled=True),
        preferred_element_type=jnp.float32,
    )
    merged = lax.psum_scatter(
        merge_terms.astype(jnp.bfloat16), "gy", scatter_dimension=1, tiled=True
    )
    pooled = lax.all_gather(merged[None], "row", axis=0, tiled=True)
    stacked = pooled.reshape(-1, merged.shape[1])
    returned = stacked[sources[0]]
    return (after_mlp[None], returned[None])


def solution(mesh):
    placed = (
        P("row", "gx", "gy"),
        P("row", None),
        P(),
        P("gx", "gy"),
        P("gx", "gy"),
        P("gx", "gy"),
        P("gy", None),
        P(),
        P("gx", "gy"),
        P("gy", "gx"),
        P(None, "gy", "gx"),
        P("row", "gx", None),
        P("row", "gx"),
    )
    return jax.shard_map(
        body,
        mesh=mesh,
        in_specs=placed,
        out_specs=(P("row", "gx", "gy"), P("row", "gx", "gy")),
        check_vma=False,
    )
```

profile of v0, /device:TPU:1, one launch (start us, length us, event | category | flops | bytes accessed | tf_op | source)
XLA Modules:
  0.0 533.2 jit_solution(15735608365847119972)
XLA Ops:
  7.2 0.7 all-gather.21.cloned.1.call-update
  8.0 0.8 reduce.7
  8.7 0.8 constant_dynamic-slice_fusion
  9.5 26.5 %all_gather.37 = bf16[1664,104]{1,0:T(8,128)(2,1)S(1)} all-gather(bf16[208,104]{1,0:T(8,128)(2,1)} %param.19), channel_id=1, replica_groups=mesh['gx'=8,'gy'=16,'row'=4] {'gx'}, dimensions={0}, use_global_device_ids=true | all-gather | bytes 389376 | tf_op jit(solution)/shard_map/all_gather | solution.py:46
  36.0 22.0 %all_gather.40 = bf16[1664,104]{1,0:T(8,128)(2,1)} all-gather(bf16[208,104]{1,0:T(8,128)(2,1)} %param.20), channel_id=1, replica_groups=mesh['gx'=8,'gy'=16,'row'=4] {'gx'}, dimensions={0}, use_global_device_ids=true | all-gather | bytes 389376 | tf_op jit(solution)/shard_map/all_gather | solution.py:47
  58.0 19.0 %all_gather.39 = bf16[1664,104]{1,0:T(8,128)(2,1)S(1)} all-gather(bf16[208,104]{1,0:T(8,128)(2,1)} %param.18), channel_id=1, replica_groups=mesh['gx'=8,'gy'=16,'row'=4] {'gx'}, dimensions={0}, use_global_device_ids=true | all-gather | bytes 389376 | tf_op jit(solution)/shard_map/all_gather | solution.py:45
  76.9 1.9 convert_reduce_fusion
  78.9 0.5 fusion.28
  79.4 0.5 fusion.30
  80.0 0.4 fusion.45
  80.4 19.9 %all-gather.3 = bf16[8,448,104]{1,2,0:T(8,128)(2,1)S(1)} all-gather(bf16[1,448,104]{1,2,0:T(8,128)(2,1)S(1)} %fusion.45), channel_id=1, replica_groups=mesh['gx'=8,'gy'=16,'row'=4] {'gx'}, dimensions={0}, use_global_device_ids=true | all-gather | bytes 838656 | tf_op jit(solution)/shard_map/all_gather | solution.py:63
  100.3 1.3 copy.45
  101.6 1.4 fusion.47
  103.0 21.5 %all-gather.4 = bf16[8,448,104]{1,2,0:T(8,128)(2,1)S(1)} all-gather(bf16[1,448,104]{1,2,0:T(8,128)(2,1)S(1)} %fusion.47), channel_id=1, replica_groups=mesh['gx'=8,'gy'=16,'row'=4] {'gx'}, dimensions={0}, use_global_device_ids=true | all-gather | bytes 838656 | tf_op jit(solution)/shard_map/all_gather | solution.py:64
  124.5 0.6 copy.46
  125.1 1.9 fusion.46
  127.0 15.5 %while.18 = (s32[]{:T(128)}, f32[448,1]{0,1:T(1,128)S(1)}, f32[448,1]{0,1:T(1,128)S(1)}, f32[448,1,104]{0,2,1:T(8,128)S(1)}, s32[448]{0:T(512)S(1)}, /*index=5*/...) while((s32[]{:T(128)}, f32[448,1]{0,1:T(1,128)S(1)}, ...), condition=%wide.region_5.6_spmd.clone, body=%wide.region_2.5_spmd.clone.sunk | while | flops 86043328 | bytes 3289283 | solution.py:95
  127.1 1.2 fusion.144
  128.3 0.2 fusion.146
  128.6 0.4 fusion.148
  129.0 1.2 fusion.144
  130.2 0.2 fusion.146
  130.5 0.4 fusion.148
  131.0 1.2 fusion.144
  132.4 0.4 fusion.148
  132.9 1.2 fusion.144
  134.4 0.4 fusion.148
  134.9 1.2 fusion.144
  136.1 0.2 fusion.146
  136.3 0.4 fusion.148
  136.8 1.2 fusion.144
  138.0 0.2 fusion.146
  138.3 0.4 fusion.148
  138.7 1.2 fusion.144
  140.0 0.2 fusion.146
  140.2 0.4 fusion.148
  140.7 1.2 fusion.144
  141.9 0.2 fusion.146
  142.1 0.4 fusion.148
  142.5 0.7 divide_convert_fusion
  143.3 0.3 copy.36
  143.6 53.7 %all_to_all.19 = bf16[104,16,104]{0,2,1:T(8,128)(2,1)S(1)} all-to-all(bf16[104,16,104]{0,2,1:T(8,128)(2,1)S(1)} %bitcast.105), channel_id=1, replica_groups=mesh['gx'=8,'gy'=16,'row'=4] {'gy'}, dimensions={1} | all-to-all | bytes 692224 | tf_op jit(solution)/shard_map/all_to_all | solution.py:97
  197.3 0.4 all_to_all.17
  197.8 17.0 %all-gather.23.cloned.1.call-done = bf16[448,1,1664]{0,2,1:T(8,128)(2,1)} async-done(((bf16[448,1,104]{0,2,1:T(8,128)(2,1)}), bf16[448,1,1664]{0,2,1:T(8,128)(2,1)}) %all-gather.23.cloned.1.call-update) | async-done | bytes 1490960 | tf_op jit(solution)/shard_map/all_gather | solution.py:99
  214.8 2.5 fusion.42
  217.3 0.5 all-gather.15.cloned.1.call-update
  217.9 0.5 all-gather.17.cloned.1.call-update
  218.5 38.7 %all-gather.13.cloned.1.call-done = bf16[448,1664]{0,1:T(8,128)(2,1)} async-done(((bf16[448,104]{0,1:T(8,128)(2,1)}), bf16[448,1664]{0,1:T(8,128)(2,1)}) %all-gather.13.cloned.1.call-update) | async-done | bytes 1490960 | tf_op jit(solution)/shard_map/all_gather | solution.py:104
  257.2 1.9 convert_reduce_fusion.1
  259.2 0.5 fusion.22
  259.7 38.1 %all-gather.15.cloned.1.call-done = bf16[1664,512]{1,0:T(8,128)(2,1)} async-done(((bf16[208,512]{1,0:T(8,128)(2,1)}), bf16[1664,512]{1,0:T(8,128)(2,1)}) %all-gather.15.cloned.1.call-update) | async-done | bytes 1703952 | tf_op jit(solution)/shard_map/all_gather | solution.py:109
  297.8 43.8 %all-gather.17.cloned.1.call-done = bf16[512,1664]{0,1:T(8,128)(2,1)} async-done(((bf16[512,208]{0,1:T(8,128)(2,1)}), bf16[512,1664]{0,1:T(8,128)(2,1)}) %all-gather.17.cloned.1.call-update) | async-done | bytes 1703952 | tf_op jit(solution)/shard_map/all_gather | solution.py:114
  341.6 7.3 %convolution_convert_fusion = bf16[448,1664]{0,1:T(8,128)(2,1)} fusion(bf16[512,1664]{0,1:T(8,128)(2,1)} %all-gather.17.cloned.1.call-done, bf16[1664,512]{1,0:T(8,128)(2,1)} %all-gather.15.cloned.1.call-done, bf16[448,1664]{0,1:T(8,128)(2,1)S(1)} %copy-done.1, f32[1664]{0:T(1024)S(1)} %copy-done.10, f32[448]{0:T(512)S(1)} %add_rsqrt_fusion, ...), kind=kOutput, calls=%fused_computation.43 | convolution fusion | flops 1546108928 | bytes 6400000 | tf_op jit(solution)/shard_map/dot_general | solution.py:113
  349.0 0.9 copy-done.7
  349.9 0.8 copy.40
  351.0 59.2 %reduce-scatter.5.cloned.1.call-done = bf16[448,104]{0,1:T(8,128)(2,1)} async-done(((bf16[448,1664]{0,1:T(8,128)(2,1)}), bf16[448,104]{0,1:T(8,128)(2,1)}) %reduce-scatter.5.cloned.1.call-update) | async-done | bytes 93200 | tf_op jit(solution)/shard_map/reduce_scatter | solution.py:116
  410.3 0.9 add_convert_fusion
  411.4 1.5 gather_fusion
  412.9 40.3 %all-gather.19.cloned.1.call-done = bf16[4,104,1664]{1,2,0:T(8,128)(2,1)} async-done(((bf16[4,104,208]{1,2,0:T(8,128)(2,1)}), bf16[4,104,1664]{1,2,0:T(8,128)(2,1)}) %all-gather.19.cloned.1.call-update) | async-done | bytes 1384464 | tf_op jit(solution)/shard_map/all_gather | solution.py:124
  453.2 2.8 fusion.31
  456.1 59.5 %reduce-scatter.7.cloned.1.call-done = bf16[112,104]{0,1:T(8,128)(2,1)} async-done(((bf16[112,1664]{0,1:T(8,128)(2,1)}), bf16[112,104]{0,1:T(8,128)(2,1)}) %reduce-scatter.7.cloned.1.call-update) | async-done | bytes 23312
  515.6 9.3 %all-gather.5 = bf16[4,112,104]{1,2,0:T(8,128)(2,1)S(1)} all-gather(bf16[1,112,104]{1,2,0:T(8,128)(2,1)} %bitcast.119), channel_id=4, replica_groups=mesh['gx'=8,'gy'=16,'row'=4] {'row'}, dimensions={0}, use_global_device_ids=true | all-gather | bytes 116480 | tf_op jit(solution)/shard_map/all_gather | solution.py:130
  524.9 0.7 gather_fusion.1
  525.6 0.7 copy.44
  (87 shorter events, 2.4 us)
Async XLA Ops:
  7.2 69.8 %all-gather.21.cloned.1.call-start = ((), (), s32[]{:S(2)}) async-start(), calls=%async_computation.8 | async-start | bytes 1810432 | tf_op jit(solution)/shard_map/all_gather | solution.py:42
  7.9 206.9 %all-gather.23.cloned.1.call-start = ((), (), s32[]{:S(2)}) async-start(), calls=%async_computation.9 | async-start | bytes 1810432 | tf_op jit(solution)/shard_map/all_gather | solution.py:99
  76.9 2.0 copy-start
  76.9 2.5 copy-start.8
  80.0 21.6 %copy-start.2 = (bf16[448,1664]{0,1:T(8,128)(2,1)}, bf16[448,1664]{0,1:T(8,128)(2,1)S(1)}, u32[]{:S(2)}) copy-start(bf16[448,1664]{0,1:T(8,128)(2,1)S(1)} %fusion.30) | copy-start | bytes 4472836
  127.0 16.3 %copy-start.6 = (bf16[104,1664]{1,0:T(8,128)(2,1)S(1)}, bf16[104,1664]{1,0:T(8,128)(2,1)}, u32[]{:S(2)}) copy-start(bf16[104,1664]{1,0:T(8,128)(2,1)} %param.21) | copy-start | bytes 1038340
  143.2 71.6 %copy-start.4 = (bf16[1,448,104]{1,2,0:T(8,128)(2,1)S(1)}, bf16[1,448,104]{1,2,0:T(8,128)(2,1)}, u32[]{:S(2)}) copy-start(bf16[1,448,104]{1,2,0:T(8,128)(2,1)} %param.15) | copy-start | bytes 279556
  143.2 114.0 %all-gather.13.cloned.1.call-start = ((), (), s32[]{:S(2)}) async-start(), calls=%async_computation.3 | async-start | bytes 1810432 | tf_op jit(solution)/shard_map/all_gather | solution.py:104
  217.3 80.5 %all-gather.15.cloned.1.call-start = ((), (), s32[]{:S(2)}) async-start(), calls=%async_computation.4 | async-start | bytes 1916928 | tf_op jit(solution)/shard_map/all_gather | solution.py:109
  217.9 123.8 %all-gather.17.cloned.1.call-start = ((), (), s32[]{:S(2)}) async-start(), calls=%async_computation.5 | async-start | bytes 1916928 | tf_op jit(solution)/shard_map/all_gather | solution.py:114
  217.9 123.7 %copy-start.10 = (f32[1664]{0:T(1024)S(1)}, f32[1664]{0:T(1024)}, u32[]{:S(2)}) copy-start(f32[1664]{0:T(1024)} %param.22) | copy-start | bytes 19972
  218.5 191.8 %reduce-scatter.5.cloned.1.call-start = ((), (), s32[]{:S(2)}) async-start(), calls=%async_computation.6 | async-start | bytes 1810432 | tf_op jit(solution)/shard_map/reduce_scatter | solution.py:116
  257.2 2.0 copy-start.1
  349.0 0.9 copy-start.7
  349.0 1.8 copy-start.9
  349.0 61.3 %copy-start.3 = (bf16[448,104]{0,1:T(8,128)(2,1)S(1)}, bf16[448,104]{0,1:T(8,128)(2,1)}, u32[]{:S(2)}) copy-start(bf16[448,104]{0,1:T(8,128)(2,1)} %fusion.42) | copy-start | bytes 279556
  349.0 104.2 %all-gather.19.cloned.1.call-start = ((), (), s32[]{:S(2)}) async-start(), calls=%async_computation.7 | async-start | bytes 1916928 | tf_op jit(solution)/shard_map/all_gather | solution.py:124
  350.7 164.8 %reduce-scatter.7.cloned.1.call-start = ((), (), s32[]{:S(2)}) async-start(), calls=%async_computation.10 | async-start | bytes 452608
  411.2 44.8 %copy-start.5 = (bf16[448,104]{0,1:T(8,128)(2,1)}, bf16[448,104]{0,1:T(8,128)(2,1)S(1)}, u32[]{:S(2)}) copy-start(bf16[448,104]{0,1:T(8,128)(2,1)S(1)} %add_convert_fusion) | copy-start | bytes 279556
  411.3 44.7 %copy-start.11 = (s32[1,112]{1,0:T(1,128)S(1)}, s32[1,112]{1,0:T(1,128)}, u32[]{:S(2)}) copy-start(s32[1,112]{1,0:T(1,128)} %param.27) | copy-start | bytes 1348
Sparse Core Ops, SparseCore 0:
  10.1 47.3 all-gather.20
  143.3 71.3 all-gather.22
  217.5 39.7 all-gather.12
  259.2 38.5 all-gather.14
  299.7 41.8 all-gather.16
  349.1 61.1 reduce-scatter.4
  412.6 40.5 all-gather.18
  456.2 59.2 reduce-scatter.6
where the time goes:
time: 538 us; the launch traced here: 533 us
  waiting for transfers between devices  298 us (55%)
  blocking collectives  172 us (32%)
  matrix products  28.8 us (5%)
  between operations  14.4 us (3%)
  other arithmetic  9.81 us (2%)
  local copies, waits for them, and re-layouts  9.22 us (2%)
    unnamed x9, waiting for transfers between devices  61.3 us
    reduce_scatter x1, waiting for transfers between devices, body(): lax.psum_scatter(partials.astype(jnp.bfloat16), 'gy', scatter_dimension=1...  59.2 us
    all_to_all x1, blocking collectives, body(): lax.all_to_all(w_out, 'gy', split_axis=1, concat_axis=0, tiled=True)  53.7 us
    all_gather x1, waiting for transfers between devices, body(): lax.all_gather(w_down, 'gx', axis=1, tiled=True)  43.8 us
    all_gather x1, waiting for transfers between devices, body(): lax.all_gather(w_merge, 'gx', axis=2, tiled=True)  40.3 us
    all_gather x1, waiting for transfers between devices, body(): gathered_mlp = lax.all_gather(after_attn, 'gy', axis=1, tiled=True)  38.7 us
    all_gather x1, waiting for transfers between devices, body(): lax.all_gather(w_up, 'gx', axis=0, tiled=True)  38.1 us
    all_gather x1, blocking collectives, body(): lax.all_gather(w_key, 'gx', axis=0, tiled=True)  26.5 us
  transfers between devices with their start and end apart: 8, of which 7 were waited for; matrix products, arithmetic and copies ran while one was open for 1% of the time, Pallas kernels for 0%

commit v1 on v0

v1 whole, which is shorter than its diff:
```python
import functools

import jax
import jax.numpy as jnp
from jax import lax
from jax.experimental import pallas as pl
from jax.experimental.pallas import tpu as pltpu
from jax.sharding import PartitionSpec as P

MESH = pl.DeviceIdType.MESH
F32 = jnp.float32
BF16 = jnp.bfloat16
EPS = 1e-06
NEG = -1e30

TOK = 448
HD = 104
SLOTS = 16
NZ = 8
NY = 8
D = 1664
FF_DEV = 512
GROUPS = 112
SCALE = HD ** (-0.5)

SEM_COUNTS = dict(
    loc=7,
    tok_y=14,
    tok_s=8,
    att_y=14,
    att_s=8,
    aft_y=14,
    aft_s=8,
    kv=14,
    qkv=14,
    wup=14,
    wdn=14,
    wmg=14,
    wo=15,
    rs_s=8,
    rs_y=7,
    mg_s=1,
    mg_y=7,
    row=3,
)


def erf_gelu(v):
    return 0.5 * v * (1.0 + lax.erf(v * (0.5 ** 0.5)))


def kernel(
    tok_h,
    seg_ref,
    ga_ref,
    wq_h,
    wk_h,
    wv_h,
    wo_ref,
    gm_ref,
    wu_h,
    wd_h,
    wm_h,
    mg_ref,
    src_ref,
    lo_ref,
    ret_ref,
    tok,
    xn,
    wqkv,
    qs,
    kv,
    att,
    aft,
    wout_s,
    wout,
    wup,
    wdn,
    wmg,
    hid,
    pp,
    sb,
    ra,
    rb,
    pk,
    mm,
    sm,
    rm,
    stk,
    seg8,
    qseg,
    gsa,
    gsm,
    m_s,
    l_s,
    acc_s,
    *sems,
):
    gx = lax.axis_index("gx")
    gy = lax.axis_index("gy")
    row = lax.axis_index("row")
    core = lax.rem(gy, 2)
    ypos = gy // 2
    d_a = 1 - 2 * core
    d_w = 1 - 2 * lax.rem(row + core, 2)

    names = list(SEM_COUNTS)
    send = {n: sems[2 * i] for i, n in enumerate(names)}
    recv = {n: sems[2 * i + 1] for i, n in enumerate(names)}

    def gy_at(delta):
        return lax.rem(gy + delta + 32, 16)

    def gx_at(delta):
        return lax.rem(gx + delta + 16, 8)

    def row_at(delta):
        return lax.rem(row + delta + 4, 4)

    def y_at(delta):
        return lax.rem(ypos + delta + 16, 8)

    sib = gy + 1 - 2 * core
    pending = []

    def push(name, idx, src, dst, target):
        copy = pltpu.make_async_remote_copy(
            src_ref=src,
            dst_ref=dst,
            send_sem=send[name].at[idx],
            recv_sem=recv[name].at[idx],
            device_id=target,
            device_id_type=MESH,
        )
        copy.start()
        pending.append(copy)

    def arrive(name, idx, ref):
        pltpu.make_async_remote_copy(
            src_ref=ref,
            dst_ref=ref,
            send_sem=send[name].at[idx],
            recv_sem=recv[name].at[idx],
            device_id={"gy": sib},
            device_id_type=MESH,
        ).wait_recv()

    local = []
    for i, (src, dst) in enumerate(
        (
            (tok_h, tok.at[gy]),
            (wq_h, wqkv.at[gx, 0]),
            (wk_h, wqkv.at[gx, 1]),
            (wv_h, wqkv.at[gx, 2]),
            (wu_h, wup.at[gx]),
            (wd_h, wdn.at[gx]),
            (wm_h, wmg.at[gx]),
        )
    ):
        copy = pltpu.make_async_copy(src, dst, send["loc"].at[i])
        copy.start()
        local.append(copy)

    barrier = pltpu.get_barrier_semaphore()
    for d in range(1, 16):
        pl.semaphore_signal(barrier, inc=1, device_id={"gy": gy_at(d)}, device_id_type=MESH)
    for d in (1, -1):
        pl.semaphore_signal(barrier, inc=1, device_id={"gx": gx_at(d)}, device_id_type=MESH)
    for d in (1, 2, 3):
        pl.semaphore_signal(barrier, inc=1, device_id={"row": row_at(d)}, device_id_type=MESH)
    pl.semaphore_wait(barrier, 20)

    half = TOK // 2

    class GatherY:
        def __init__(self, name, buf):
            self.name, self.buf = name, buf

        def part(self, slot, ch):
            return self.buf.at[slot, pl.ds(ch * half, half)]

        def ahead(self, s, ch):
            slot = gy_at(-2 * (s - 1) * d_a)
            ref = self.part(slot, ch)
            push(self.name + "_y", 2 * (s - 1) + ch, ref, ref, {"gy": gy_at(2 * d_a)})

        def back(self, s, ch):
            slot = gy_at(2 * (s - 1) * d_a)
            ref = self.part(slot, ch)
            push(self.name + "_y", 8 + 2 * (s - 1) + ch, ref, ref, {"gy": gy_at(-2 * d_a)})

        def across(self, idx, slot):
            ref = self.buf.at[slot]
            push(self.name + "_s", idx, ref, ref, {"gy": sib})

        def start(self):
            for ch in (0, 1):
                self.ahead(1, ch)
                self.back(1, ch)
            self.across(0, gy)

        def step(self, s):
            slot_a = gy_at(-2 * s * d_a)
            slot_b = gy_at(2 * s * d_a)
            for ch in (0, 1):
                arrive(self.name + "_y", 2 * (s - 1) + ch, self.part(slot_a, ch))
                if s < 4:
                    self.ahead(s + 1, ch)
                if s < 4:
                    arrive(self.name + "_y", 8 + 2 * (s - 1) + ch, self.part(slot_b, ch))
                    if s < 3:
                        self.back(s + 1, ch)
            self.across(s, slot_a)
            if s < 4:
                self.across(4 + s, slot_b)

        def finish(self):
            arrive(self.name + "_s", 0, self.buf.at[sib])
            for s in range(1, 5):
                arrive(self.name + "_s", s, self.buf.at[lax.rem(sib + 2 * s * d_a + 32, 16)])
                if s < 4:
                    arrive(self.name + "_s", 4 + s, self.buf.at[lax.rem(sib - 2 * s * d_a + 32, 16)])

    class Weights:
        def __init__(self, name, buf, parts):
            self.name, self.buf, self.parts = name, buf, parts

        def ref(self, slot, p):
            return self.parts(self.buf, slot, p)

        def ahead(self, s):
            slot = gx_at(-(s - 1) * d_w)
            for p in (0, 1):
                ref = self.ref(slot, p)
                push(self.name, 2 * (s - 1) + p, ref, ref, {"gx": gx_at(d_w)})

        def step(self, s):
            slot = gx_at(-s * d_w)
            for p in (0, 1):
                ref = self.ref(slot, p)
                arrive(self.name, 2 * (s - 1) + p, ref)
                if s < 4:
                    push(self.name, 2 * s + p, ref, ref, {"gx": gx_at(d_w)})
                    side = d_a if p == 0 else -d_a
                    push(self.name, 8 + 2 * (s - 1) + p, ref, ref, {"row": row_at(side)})

        def finish(self):
            for s in (1, 2, 3):
                for p in (0, 1):
                    arrive(self.name, 8 + 2 * (s - 1) + p, self.ref(gx_at(s * d_w), p))

    def cut(at, end):
        def parts(buf, slot, p):
            return buf.at[slot, pl.ds(0, at)] if p == 0 else buf.at[slot, pl.ds(at, end - at)]

        return parts

    g_tok = GatherY("tok", tok)
    g_att = GatherY("att", att)
    g_aft = GatherY("aft", aft)
    w_qkv = Weights("qkv", wqkv, cut(2, 3))
    w_up = Weights("wup", wup, cut(112, 208))
    w_dn = Weights("wdn", wdn, cut(256, 512))
    w_mg = Weights("wmg", wmg, cut(2, 4))

    local[0].wait()
    g_tok.start()
    for i in (1, 2, 3):
        local[i].wait()
    w_qkv.ahead(1)

    for j in range(SLOTS):
        wout_s[j] = wo_ref[:, j * HD : (j + 1) * HD]
        gsa[j] = ga_ref[:, j * HD : (j + 1) * HD]
        gsm[j] = gm_ref[:, j * HD : (j + 1) * HD]
    for j in range(NZ):
        seg8[j : j + 1, :] = seg_ref[:, j * TOK : (j + 1) * TOK]
    own_row = seg8[pl.ds(gx, 1), :]
    eye = lax.broadcasted_iota(jnp.int32, (TOK, TOK), 0) == lax.broadcasted_iota(
        jnp.int32, (TOK, TOK), 1
    )
    qseg[...] = jnp.sum(jnp.where(eye, own_row.astype(F32), 0.0), axis=1, keepdims=True)

    for s in (1, 2, 3, 4):
        g_tok.step(s)
        w_qkv.step(s)
    g_tok.finish()

    def norm(src, gains, out):
        rows = 64

        def chunk(r, carry):
            at = pl.ds(pl.multiple_of(r * rows, rows), rows)
            total = src[0, at, :].astype(F32)
            for j in range(1, SLOTS):
                total += src[j, at, :].astype(F32)
            mean = jnp.sum(total, axis=-1, keepdims=True) * (1.0 / D)
            square = jnp.zeros((rows, HD), F32)
            for j in range(SLOTS):
                gap = src[j, at, :].astype(F32) - mean
                square += gap * gap
            var = jnp.sum(square, axis=-1, keepdims=True) * (1.0 / D)
            rstd = lax.rsqrt(var + EPS)
            for j in range(SLOTS):
                gap = src[j, at, :].astype(F32) - mean
                out[j // 2, at, (j % 2) * HD : (j % 2 + 1) * HD] = (gap * rstd * gains[j]).astype(BF16)
            return carry

        lax.fori_loop(0, TOK // rows, chunk, 0)

    norm(tok, gsa, xn)
    w_qkv.finish()

    rows2 = TOK // 2

    def project(r, carry):
        at = pl.ds(pl.multiple_of(r * rows2, rows2), rows2)
        for m in (1, 2, 0):
            total = jnp.zeros((rows2, HD), F32)
            for j in range(NZ):
                total += jnp.dot(xn[j, at, :], wqkv[j, m], preferred_element_type=F32)
            if m == 0:
                qs[at, :] = total.astype(BF16)
            else:
                kv[gx, m - 1, at, :] = total.astype(BF16)
        return carry

    lax.fori_loop(0, 2, project, 0)

    def kv_ahead(s):
        slot = gx_at(-(s - 1) * d_a)
        for p in (0, 1):
            ref = kv.at[slot, p]
            push("kv", 2 * (s - 1) + p, ref, ref, {"gx": gx_at(d_a)})

    def kv_back(s):
        slot = gx_at((s - 1) * d_a)
        for p in (0, 1):
            ref = kv.at[slot, p]
            push("kv", 8 + 2 * (s - 1) + p, ref, ref, {"gx": gx_at(-d_a)})

    kv_ahead(1)
    kv_back(1)
    local[4].wait()
    w_up.ahead(1)
    for d in range(1, 16):
        to = gy_at(d)
        push("wo", d - 1, wout_s.at[to], wout.at[gy], {"gy": to})
    wout[gy] = wout_s[gy]

    rows4 = TOK // 4

    def attend(block, first):
        key_seg = seg8[pl.ds(block, 1), :].astype(F32)

        def chunk(r, carry):
            at = pl.ds(pl.multiple_of(r * rows4, rows4), rows4)
            scores = (
                lax.dot_general(
                    qs[at, :], kv[block, 0], (((1,), (1,)), ((), ())), preferred_element_type=F32
                )
                * SCALE
            )
            scores = jnp.where(qseg[at, :] == key_seg, scores, NEG)
            top = jnp.max(scores, axis=-1, keepdims=True)
            if not first:
                old_top = m_s[at, :]
                top = jnp.maximum(old_top, top)
            weights = jnp.exp(scores - top)
            total = jnp.sum(weights, axis=-1, keepdims=True)
            mixed = jnp.dot(weights.astype(BF16), kv[block, 1], preferred_element_type=F32)
            if not first:
                fade = jnp.exp(old_top - top)
                total += l_s[at, :] * fade
                mixed += acc_s[at, :] * fade
            m_s[at, :] = top
            l_s[at, :] = total
            acc_s[at, :] = mixed
            return carry

        lax.fori_loop(0, TOK // rows4, chunk, 0)

    attend(gx, True)
    for s in (1, 2, 3, 4):
        slot_a, slot_b = gx_at(-s * d_a), gx_at(s * d_a)
        for p in (0, 1):
            arrive("kv", 2 * (s - 1) + p, kv.at[slot_a, p])
            if s < 4:
                ref = kv.at[slot_a, p]
                push("kv", 2 * s + p, ref, ref, {"gx": gx_at(d_a)})
            if s < 4:
                arrive("kv", 8 + 2 * (s - 1) + p, kv.at[slot_b, p])
                if s < 3:
                    ref = kv.at[slot_b, p]
                    push("kv", 8 + 2 * s + p, ref, ref, {"gx": gx_at(-d_a)})
        attend(slot_a, False)
        if s < 4:
            attend(slot_b, False)
        w_up.step(s)

    att[gy] = (acc_s[...] / l_s[...]).astype(BF16)
    g_att.start()
    local[5].wait()
    w_dn.ahead(1)
    for d in range(1, 16):
        arrive("wo", d - 1, wout.at[gy_at(-d)])
    for s in (1, 2, 3, 4):
        g_att.step(s)
        w_dn.step(s)
    g_att.finish()

    def out_proj(r, carry):
        at = pl.ds(pl.multiple_of(r * rows2, rows2), rows2)
        total = jnp.zeros((rows2, HD), F32)
        for j in range(SLOTS):
            total += jnp.dot(att[j, at, :], wout[j], preferred_element_type=F32)
        aft[gy, at, :] = (tok[gy, at, :].astype(F32) + total).astype(BF16)
        return carry

    lax.fori_loop(0, 2, out_proj, 0)

    g_aft.start()
    local[6].wait()
    w_mg.ahead(1)
    for s in (1, 2, 3, 4):
        g_aft.step(s)
        w_mg.step(s)
    g_aft.finish()
    norm(aft, gsm, xn)
    w_up.finish()

    def mlp_up(r, carry):
        at = pl.ds(pl.multiple_of(r * rows4, rows4), rows4)
        total = jnp.zeros((rows4, FF_DEV), F32)
        for j in range(NZ):
            total += jnp.dot(xn[j, at, :], wup[j], preferred_element_type=F32)
        hid[at, :] = erf_gelu(total).astype(BF16)
        return carry

    lax.fori_loop(0, 4, mlp_up, 0)
    w_dn.finish()

    order = (4, -3, 3, -2, 2, -1, 1, 0)
    for i, d in enumerate(order):
        dest = y_at(d * d_a)
        for h in (0, 1):
            pass

        def mlp_down(r, carry):
            at = pl.ds(pl.multiple_of(r * rows2, rows2), rows2)
            part = jnp.dot(hid[at, :], wdn[dest], preferred_element_type=F32)
            pp[dest, 0, at, :] = part[:, :HD].astype(BF16)
            pp[dest, 1, at, :] = part[:, HD:].astype(BF16)
            return carry

        lax.fori_loop(0, 2, mlp_down, 0)
        push("rs_s", i, pp.at[dest, 1 - core], sb.at[dest], {"gy": sib})

    def fold(dest, extra):
        pp[dest, core] = (pp[dest, core].astype(F32) + extra.astype(F32)).astype(BF16)

    for i, d in enumerate(order):
        arrive("rs_s", i, sb.at[y_at(-d * d_a)])

    def fold_all(j, carry):
        fold(j, sb[j])
        return carry

    lax.fori_loop(0, NY, fold_all, 0)
    ahead, behind = {"gy": gy_at(2 * d_a)}, {"gy": gy_at(-2 * d_a)}
    push("rs_y", 0, pp.at[y_at(4 * d_a), core], ra.at[0], ahead)
    push("rs_y", 4, pp.at[y_at(-3 * d_a), core], rb.at[0], behind)
    for s in (1, 2, 3):
        arrive("rs_y", s - 1, ra.at[s - 1])
        dest = y_at((4 - s) * d_a)
        fold(dest, ra[s - 1])
        push("rs_y", s, pp.at[dest, core], ra.at[s], ahead)
        if s < 3:
            arrive("rs_y", 4 + s - 1, rb.at[s - 1])
            dest = y_at(-(3 - s) * d_a)
            fold(dest, rb[s - 1])
            push("rs_y", 4 + s, pp.at[dest, core], rb.at[s], behind)
    arrive("rs_y", 6, rb.at[2])
    arrive("rs_y", 3, ra.at[3])
    lo_ref[...] = (
        aft[gy].astype(F32)
        + (pp[ypos, core].astype(F32) + ra[3].astype(F32) + rb[2].astype(F32))
    ).astype(BF16)

    w_mg.finish()
    spot = lax.broadcasted_iota(jnp.int32, (GROUPS, TOK), 1)
    for k in range(4):
        pick = jnp.where(mg_ref[:, k : k + 1] == spot, 1.0, 0.0).astype(BF16)
        pk[k] = jnp.dot(pick, lo_ref[...], preferred_element_type=F32).astype(BF16)

    def merge(j, carry):
        total = jnp.zeros((GROUPS, 2 * HD), F32)
        for k in range(4):
            total += jnp.dot(pk[k], wmg[j, k], preferred_element_type=F32)
        mm[0, j] = total[:, :HD].astype(BF16)
        mm[1, j] = total[:, HD:].astype(BF16)
        return carry

    lax.fori_loop(0, NY, merge, 0)
    push("mg_s", 0, mm.at[1 - core], sm, {"gy": sib})
    arrive("mg_s", 0, sm)
    mm[core] = (mm[core].astype(F32) + sm[...].astype(F32)).astype(BF16)
    for d in (4, 3, 5, 2, 6, 1, 7):
        push("mg_y", d - 1, mm.at[core, y_at(d)], rm.at[d - 1], {"gy": gy_at(2 * d)})
    total = mm[core, ypos].astype(F32)
    for d in range(1, 8):
        arrive("mg_y", d - 1, rm.at[d - 1])
    for d in range(1, 8):
        total += rm[d - 1].astype(F32)
    stk[row] = total.astype(BF16)
    for d in (1, 2, 3):
        push("row", d - 1, stk.at[row], stk.at[row], {"row": row_at(d)})
    eye2 = lax.broadcasted_iota(jnp.int32, (GROUPS, GROUPS), 0) == lax.broadcasted_iota(
        jnp.int32, (GROUPS, GROUPS), 1
    )
    wanted = jnp.sum(jnp.where(eye2, src_ref[...].astype(F32), 0.0), axis=1, keepdims=True)
    for d in (1, 2, 3):
        arrive("row", d - 1, stk.at[row_at(-d)])
    place = lax.broadcasted_iota(jnp.int32, (GROUPS, GROUPS), 1).astype(F32)
    total = jnp.zeros((GROUPS, HD), F32)
    for r in range(4):
        pick = jnp.where(wanted == place + float(GROUPS * r), 1.0, 0.0).astype(BF16)
        total += jnp.dot(pick, stk[r], preferred_element_type=F32)
    ret_ref[...] = total.astype(BF16)

    for copy in pending:
        copy.wait_send()


def body(
    tokens,
    segments,
    gain_attn,
    w_query,
    w_key,
    w_value,
    w_out,
    gain_mlp,
    w_up,
    w_down,
    w_merge,
    merge_groups,
    sources,
):
    anyspace = pl.BlockSpec(memory_space=pl.ANY)
    vmem = pl.BlockSpec(memory_space=pltpu.VMEM)
    scratch = [
        pltpu.VMEM((SLOTS, TOK, HD), BF16),
        pltpu.VMEM((NZ, TOK, 2 * HD), BF16),
        pltpu.VMEM((NZ, 3, 2 * HD, HD), BF16),
        pltpu.VMEM((TOK, HD), BF16),
        pltpu.VMEM((NZ, 2, TOK, HD), BF16),
        pltpu.VMEM((SLOTS, TOK, HD), BF16),
        pltpu.VMEM((SLOTS, TOK, HD), BF16),
        pltpu.VMEM((SLOTS, HD, HD), BF16),
        pltpu.VMEM((SLOTS, HD, HD), BF16),
        pltpu.VMEM((NZ, 2 * HD, FF_DEV), BF16),
        pltpu.VMEM((NZ, FF_DEV, 2 * HD), BF16),
        pltpu.VMEM((NZ, 4, HD, 2 * HD), BF16),
        pltpu.VMEM((TOK, FF_DEV), BF16),
        pltpu.VMEM((NY, 2, TOK, HD), BF16),
        pltpu.VMEM((NY, TOK, HD), BF16),
        pltpu.VMEM((4, TOK, HD), BF16),
        pltpu.VMEM((3, TOK, HD), BF16),
        pltpu.VMEM((4, GROUPS, HD), BF16),
        pltpu.VMEM((2, NY, GROUPS, HD), BF16),
        pltpu.VMEM((NY, GROUPS, HD), BF16),
        pltpu.VMEM((7, GROUPS, HD), BF16),
        pltpu.VMEM((4, GROUPS, HD), BF16),
        pltpu.VMEM((NZ, TOK), jnp.int32),
        pltpu.VMEM((TOK, 1), F32),
        pltpu.VMEM((SLOTS, 1, HD), F32),
        pltpu.VMEM((SLOTS, 1, HD), F32),
        pltpu.VMEM((TOK, 1), F32),
        pltpu.VMEM((TOK, 1), F32),
        pltpu.VMEM((TOK, HD), F32),
    ]
    for count in SEM_COUNTS.values():
        scratch += [pltpu.SemaphoreType.DMA((count,)), pltpu.SemaphoreType.DMA((count,))]
    layer_out, returned = pl.pallas_call(
        kernel,
        out_shape=(
            jax.ShapeDtypeStruct((TOK, HD), BF16),
            jax.ShapeDtypeStruct((GROUPS, HD), BF16),
        ),
        in_specs=[
            anyspace,
            vmem,
            vmem,
            anyspace,
            anyspace,
            anyspace,
            vmem,
            vmem,
            anyspace,
            anyspace,
            anyspace,
            vmem,
            vmem,
        ],
        out_specs=(vmem, vmem),
        scratch_shapes=scratch,
        compiler_params=pltpu.CompilerParams(
            collective_id=0, has_side_effects=True, vmem_limit_bytes=48 << 20
        ),
        name="layer",
    )(
        tokens[0],
        segments,
        gain_attn.reshape(1, D),
        w_query,
        w_key,
        w_value,
        w_out,
        gain_mlp.reshape(1, D),
        w_up,
        w_down,
        w_merge,
        merge_groups[0],
        sources,
    )
    return (layer_out[None], returned[None])


def solution(mesh):
    placed = (
        P("row", "gx", "gy"),
        P("row", None),
        P(),
        P("gx", "gy"),
        P("gx", "gy"),
        P("gx", "gy"),
        P("gy", None),
        P(),
        P("gx", "gy"),
        P("gy", "gx"),
        P(None, "gy", "gx"),
        P("row", "gx", None),
        P("row", "gx"),
    )
    return jax.shard_map(
        body,
        mesh=mesh,
        in_specs=placed,
        out_specs=(P("row", "gx", "gy"), P("row", "gx", "gy")),
        check_vma=False,
    )
```

time: 538 us -> 161 us (0.30)
  waiting for transfers between devices: 298 us -> 0 us
  blocking collectives: 172 us -> 0 us
  Pallas kernels: 0 us -> 152 us
  matrix products: 28.8 us -> 0 us
  between operations: 14.4 us -> 0.74 us
  other arithmetic: 9.81 us -> 0 us
    all_gather x6 -> x0, waiting for transfers between devices: 178 us -> none  [the longest x1 43.8 us: body(): lax.all_gather(w_down, 'gx', axis=1, tiled=True)]
    pallas_call x0 -> x1, Pallas kernels: none -> 152 us  [body(): pl.pallas_call(kernel, out_shape=(jax.ShapeDtypeStruct((TOK, HD), BF16),...]
    all_gather x6 -> x0, blocking collectives: 118 us -> none  [the longest x1 26.5 us: body(): lax.all_gather(w_key, 'gx', axis=0, tiled=True)]
    unnamed x9 -> x0, waiting for transfers between devices: 61.3 us -> none
    reduce_scatter x1 -> x0, waiting for transfers between devices: 59.2 us -> none  [body(): lax.psum_scatter(partials.astype(jnp.bfloat16), 'gy', scatter_dimension=1...]
    all_to_all x1 -> x0, blocking collectives: 53.7 us -> none  [body(): lax.all_to_all(w_out, 'gy', split_axis=1, concat_axis=0, tiled=True)]
    dot_general x22 -> x0, matrix products: 28.8 us -> none  [the longest x8 9.48 us: one_block(): jnp.einsum('qhd,khd->qhk', queries, key_heads, preferred_element_type=jnp...]
    reduce_sum x12 -> x0, other arithmetic: 6.68 us -> none  [the longest x2 3.84 us: normalize(): row_mean = jnp.mean(tok_rows, axis=-1, keepdims=True)]
  transfers between devices with their start and end apart: 8 -> 0, of which waited for: 7 -> 0; matrix products, arithmetic and copies ran while one was open for 1% -> 0% of each run, Pallas kernels for 0% -> 0%
where the time goes in v1:
time: 161 us
  Pallas kernels  152 us (94%)
  local copies, waits for them, and re-layouts  7.66 us (5%)
    pallas_call x1, Pallas kernels, body(): pl.pallas_call(kernel, out_shape=(jax.ShapeDtypeStruct((TOK, HD), BF16),...  152 us
    unnamed x23, local copies, waits for them, and re-layouts  6.2 us

profile of v1, /device:TPU:1, one launch (start us, length us, event | category | flops | bytes accessed | tf_op | source)
XLA Modules:
  0.0 160.6 jit_solution(7136345236253597094)
XLA Ops:
  0.6 0.0 copy-start.8
  0.6 0.0 copy-start.6
  0.7 0.7 reshape.10.ga_ref
  1.4 0.0 copy-start.2
  1.4 0.7 reshape.11.gm_ref
  2.1 0.0 copy-done.8
  2.1 0.1 copy.16
  2.2 0.0 copy-start
  2.2 1.1 copy.15
  3.3 0.0 copy-start.1
  3.3 0.0 copy-start.7
  3.3 1.1 copy.17.wd_h
  4.4 0.0 copy-done.6
  4.5 0.0 copy-done.2
  4.5 0.0 copy-done
  4.5 0.0 copy-done.1
  4.5 0.0 copy-done.7
  4.5 0.0 copy-start.3
  4.5 0.8 copy-done.3
  5.3 0.0 copy-start.4
  5.3 0.8 copy-done.4
  6.1 0.0 copy-start.5
  6.1 0.8 copy-done.5
  6.9 152.2 %layer.1 = (bf16[448,104]{1,0:T(8,128)(2,1)S(1)}, bf16[112,104]{1,0:T(8,128)(2,1)S(1)}) custom-call(bf16[448,104]{1,0:T(8,128)(2,1)S(1)} %bitcast.4, s32[1,3584]{1,0:T(1,128)S(1)} %copy-done.6, f32[1,1664]{1,0:T(1,128)S(1)} %reshape.10.ga_ref, bf16[208,104]{1,0:T(8,128)(2,1)S(1)} %copy-done.3, bf16[208,104]{1,0:T(8,128)(2,1)S(1)} %copy-done.4, ...), custom_call_target="tpu_custom_call" | custom-call | tf_op jit(solution)/shard_map/layer/pallas_call | solution.py:585
  159.1 0.8 copy.18
  159.9 0.7 copy.19
Async XLA Ops:
  0.6 1.5 copy-start.8
  0.6 3.8 %copy-start.6 = (s32[1,3584]{1,0:T(1,128)S(1)}, s32[1,3584]{1,0:T(1,128)}, u32[]{:S(2)}) copy-start(s32[1,3584]{1,0:T(1,128)} %seg_ref.1) | copy-start | bytes 43012
  1.4 3.1 %copy-start.2 = (bf16[4,104,208]{2,1,0:T(8,128)(2,1)S(1)}, bf16[4,104,208]{2,1,0:T(8,128)(2,1)}, u32[]{:S(2)}) copy-start(bf16[4,104,208]{2,1,0:T(8,128)(2,1)} %wm_h.1) | copy-start | bytes 519172
  2.2 2.2 %copy-start = (bf16[104,1664]{1,0:T(8,128)(2,1)S(1)}, bf16[104,1664]{1,0:T(8,128)(2,1)}, u32[]{:S(2)}) copy-start(bf16[104,1664]{1,0:T(8,128)(2,1)} %wo_ref.1) | copy-start | bytes 1038340
  3.3 1.2 copy-start.1
  3.3 1.2 copy-start.7
  4.5 0.8 copy-start.3
  5.3 0.8 copy-start.4
  6.1 0.8 copy-start.5

commit v2 on v1

v2 whole, which is shorter than its diff:
```python
import functools

import jax
import jax.numpy as jnp
from jax import lax
from jax.experimental import pallas as pl
from jax.experimental.pallas import tpu as pltpu
from jax.sharding import PartitionSpec as P

MESH = pl.DeviceIdType.MESH
F32 = jnp.float32
BF16 = jnp.bfloat16
EPS = 1e-06
NEG = -1e30

TOK = 448
HD = 104
SLOTS = 16
NZ = 8
NY = 8
D = 1664
FF_DEV = 512
GROUPS = 112
EXP2 = HD ** (-0.5) * 1.4426950408889634

HALF = TOK // 2

LOCAL = 13
SEM_COUNTS = dict(
    tok_y=14,
    tok_s=8,
    kv=14,
    qkv=14,
    wup=7,
    wdn=7,
    wmg=7,
    bulk=2,
    wo=8,
    swap=2,
    att_y=14,
    aft_y=14,
    rs_y=14,
    mg_s=1,
    mg_y=7,
    row=3,
)


def erf_gelu(v):
    return 0.5 * v * (1.0 + lax.erf(v * (0.5 ** 0.5)))


def kernel(
    tok_h,
    seg_h,
    ga_h,
    wq_h,
    wk_h,
    wv_h,
    wo_h,
    gm_h,
    wu_h,
    wd_h,
    wm_h,
    mg_h,
    src_h,
    lo_ref,
    ret_ref,
    tok,
    xn,
    wqkv,
    qs,
    kv,
    att,
    aft,
    wout_s,
    wout,
    wup,
    wdn,
    wmg,
    hid,
    pp,
    ra,
    rb,
    lo_s,
    swap_s,
    pk,
    mm,
    sm,
    rm,
    stk,
    seg8,
    qseg,
    gsa,
    gsm,
    m_s,
    l_s,
    acc_s,
    tok_t,
    wo_ref,
    seg_ref,
    mg_ref,
    src_ref,
    ga_ref,
    gm_ref,
    loc_sem,
    *sems,
):
    gx = lax.axis_index("gx")
    gy = lax.axis_index("gy")
    row = lax.axis_index("row")
    core = lax.rem(gy, 2)
    ypos = gy // 2
    d_a = 1 - 2 * core
    d_w = 1 - 2 * lax.rem(row + core, 2)

    names = list(SEM_COUNTS)
    send = {n: sems[2 * i] for i, n in enumerate(names)}
    recv = {n: sems[2 * i + 1] for i, n in enumerate(names)}

    def gy_at(delta):
        return lax.rem(gy + delta + 32, 16)

    def gx_at(delta):
        return lax.rem(gx + delta + 16, 8)

    def row_at(delta):
        return lax.rem(row + delta + 4, 4)

    def y_at(delta):
        return lax.rem(ypos + delta + 16, 8)

    sib = gy + 1 - 2 * core
    pending = []

    def push(name, idx, src, dst, target):
        copy = pltpu.make_async_remote_copy(
            src_ref=src,
            dst_ref=dst,
            send_sem=send[name].at[idx],
            recv_sem=recv[name].at[idx],
            device_id=target,
            device_id_type=MESH,
        )
        copy.start()
        pending.append(copy)

    def arrive(name, idx, ref):
        pltpu.make_async_remote_copy(
            src_ref=ref,
            dst_ref=ref,
            send_sem=send[name].at[idx],
            recv_sem=recv[name].at[idx],
            device_id={"gy": sib},
            device_id_type=MESH,
        ).wait_recv()

    local = []
    for i, (src, dst) in enumerate(
        (
            (tok_h, tok_t),
            (wq_h, wqkv.at[gx, 0]),
            (wk_h, wqkv.at[gx, 1]),
            (wv_h, wqkv.at[gx, 2]),
            (wo_h, wo_ref),
            (seg_h, seg_ref),
            (mg_h, mg_ref),
            (src_h, src_ref),
            (ga_h, ga_ref),
            (gm_h, gm_ref),
            (wu_h, wup.at[core, gx]),
            (wd_h, wdn.at[core, gx]),
            (wm_h, wmg.at[gx]),
        )
    ):
        copy = pltpu.make_async_copy(src, dst, loc_sem.at[i])
        copy.start()
        local.append(copy)
    local[0].wait()
    tok[gy] = jnp.transpose(tok_t[...])

    barrier = pltpu.get_barrier_semaphore()
    for d in range(1, 8):
        pl.semaphore_signal(barrier, inc=1, device_id={"gy": gy_at(2 * d)}, device_id_type=MESH)
    pl.semaphore_signal(barrier, inc=1, device_id={"gy": sib}, device_id_type=MESH)
    for d in (1, -1):
        pl.semaphore_signal(barrier, inc=1, device_id={"gx": gx_at(d)}, device_id_type=MESH)
    for d in (1, 2, 3):
        pl.semaphore_signal(barrier, inc=1, device_id={"row": row_at(d)}, device_id_type=MESH)
    pl.semaphore_wait(barrier, 13)

    class Ring:
        def __init__(self, name, part):
            self.name, self.part = name, part

        def ahead(self, s, p):
            ref = self.part(-(s - 1) * d_a, p)
            push(self.name, 2 * (s - 1) + p, ref, ref, {"gy": gy_at(2 * d_a)})

        def back(self, s, p):
            ref = self.part((s - 1) * d_a, p)
            push(self.name, 8 + 2 * (s - 1) + p, ref, ref, {"gy": gy_at(-2 * d_a)})

        def start(self, p):
            self.ahead(1, p)
            self.back(1, p)

        def step(self, s):
            for p in (0, 1):
                arrive(self.name, 2 * (s - 1) + p, self.part(-s * d_a, p))
                if s < 4:
                    self.ahead(s + 1, p)
                    arrive(self.name, 8 + 2 * (s - 1) + p, self.part(s * d_a, p))
                    if s < 3:
                        self.back(s + 1, p)

    def tok_part(k, p):
        return tok.at[gy_at(2 * k), pl.ds(p * HALF, HALF)]

    def across(idx, slot):
        push("tok_s", idx, tok.at[slot], tok.at[slot], {"gy": sib})

    def pair_part(buf):
        def part(k, p):
            slot = 2 * y_at(k) + (core if p == 0 else 1 - core)
            return buf.at[slot]

        return part

    class Weights:
        def __init__(self, name, buf, cuts):
            self.name, self.buf, self.cuts = name, buf, cuts
            self.n = len(cuts)

        def ref(self, slot, p):
            at, size = self.cuts[p]
            return self.buf.at[slot, pl.ds(at, size)]

        def ahead(self):
            for p in range(self.n):
                ref = self.ref(gx, p)
                push(self.name, p, ref, ref, {"gx": gx_at(d_w)})

        def step(self, s):
            slot = gx_at(-s * d_w)
            for p in range(self.n):
                ref = self.ref(slot, p)
                arrive(self.name, self.n * (s - 1) + p, ref)
                if s < 4:
                    push(self.name, self.n * s + p, ref, ref, {"gx": gx_at(d_w)})
                    side = d_a if p % 2 == 0 else -d_a
                    push(self.name, self.n * (s + 3) + p, ref, ref, {"row": row_at(side)})

        def finish(self):
            for s in (1, 2, 3):
                for p in range(self.n):
                    arrive(self.name, self.n * (s + 3) + p, self.ref(gx_at(s * d_w), p))

    g_tok = Ring("tok_y", tok_part)
    g_att = Ring("att_y", pair_part(att))
    g_aft = Ring("aft_y", pair_part(aft))
    w_qkv = Weights("qkv", wqkv, ((0, 2), (2, 1)))
    w_up = Weights("wup", wup.at[core], ((0, 208),))
    w_dn = Weights("wdn", wdn.at[core], ((0, 208),))
    w_mg = Weights("wmg", wmg, ((0, 4),))

    g_tok.start(0)
    g_tok.start(1)
    across(0, gy)
    for i in (1, 2, 3):
        local[i].wait()
    w_qkv.ahead()
    for i in range(4, 10):
        local[i].wait()

    for j in range(SLOTS):
        gsa[j] = ga_ref[:, j * HD : (j + 1) * HD]
        gsm[j] = gm_ref[:, j * HD : (j + 1) * HD]
    for j in range(NY):
        wout_s[j] = wo_ref[:, j * 2 * HD : (j + 1) * 2 * HD]
    for j in range(NZ):
        seg8[j : j + 1, :] = seg_ref[:, j * TOK : (j + 1) * TOK]
    own_row = seg8[pl.ds(gx, 1), :]
    eye = lax.broadcasted_iota(jnp.int32, (TOK, TOK), 0) == lax.broadcasted_iota(
        jnp.int32, (TOK, TOK), 1
    )
    qseg[...] = jnp.sum(jnp.where(eye, own_row.astype(F32), 0.0), axis=1, keepdims=True)

    for s in (1, 2, 3, 4):
        g_tok.step(s)
        across(s, gy_at(-2 * s * d_a))
        if s < 4:
            across(4 + s, gy_at(2 * s * d_a))
        w_qkv.step(s)
    local[10].wait()
    w_up.ahead()
    arrive("tok_s", 0, tok.at[sib])
    for s in (1, 2, 3, 4):
        arrive("tok_s", s, tok.at[lax.rem(sib + 2 * s * d_a + 32, 16)])
        if s < 4:
            arrive("tok_s", 4 + s, tok.at[lax.rem(sib - 2 * s * d_a + 32, 16)])

    def norm(src, gains, out, count, rows):

        def chunk(r, carry):
            at = pl.ds(pl.multiple_of(r * rows, rows), rows)
            total = src[0, at, :].astype(F32)
            for j in range(1, SLOTS):
                total += src[j, at, :].astype(F32)
            mean = jnp.sum(total, axis=-1, keepdims=True) * (1.0 / D)
            square = jnp.zeros((rows, HD), F32)
            for j in range(SLOTS):
                gap = src[j, at, :].astype(F32) - mean
                square += gap * gap
            var = jnp.sum(square, axis=-1, keepdims=True) * (1.0 / D)
            rstd = lax.rsqrt(var + EPS)
            for j in range(SLOTS):
                gap = src[j, at, :].astype(F32) - mean
                out[j // 2, at, (j % 2) * HD : (j % 2 + 1) * HD] = (gap * rstd * gains[j]).astype(BF16)
            return carry

        lax.fori_loop(0, count // rows, chunk, 0)

    norm(tok, gsa, xn, TOK, 64)
    w_qkv.finish()

    rows2 = TOK // 2

    def project(m):
        def chunk(r, carry):
            at = pl.ds(pl.multiple_of(r * rows2, rows2), rows2)
            total = jnp.zeros((rows2, HD), F32)
            for j in range(NZ):
                total += jnp.dot(xn[j, at, :], wqkv[j, m], preferred_element_type=F32)
            if m == 0:
                qs[at, :] = total.astype(BF16)
            else:
                kv[gx, m - 1, at, :] = total.astype(BF16)
            return carry

        lax.fori_loop(0, 2, chunk, 0, unroll=True)

    def kv_ahead(s, p):
        ref = kv.at[gx_at(-(s - 1) * d_a), p]
        push("kv", 2 * (s - 1) + p, ref, ref, {"gx": gx_at(d_a)})

    def kv_back(s, p):
        ref = kv.at[gx_at((s - 1) * d_a), p]
        push("kv", 8 + 2 * (s - 1) + p, ref, ref, {"gx": gx_at(-d_a)})

    for p in (0, 1):
        project(p + 1)
        kv_ahead(1, p)
        kv_back(1, p)
    project(0)
    for d in range(1, 8):
        to = y_at(d)
        push("wo", d - 1, wout_s.at[to], wout.at[core, ypos], {"gy": gy_at(2 * d)})
    wout[core, ypos] = wout_s[ypos]

    rows4 = TOK // 4

    def attend(block, first=False, part=None):
        start = 0 if part is None else part * HALF
        key_seg = seg8[pl.ds(block, 1), :].astype(F32)

        def chunk(r, carry):
            at = pl.ds(pl.multiple_of(start + r * rows4, 16), rows4)
            scores = lax.dot_general(
                qs[at, :], kv[block, 0], (((1,), (1,)), ((), ())), preferred_element_type=F32
            )
            scores = jnp.where(qseg[at, :] == key_seg, scores, NEG)
            top = jnp.max(scores, axis=-1, keepdims=True)
            if not first:
                old_top = m_s[at, :]
                top = jnp.maximum(old_top, top)
            weights = jnp.exp2((scores - top) * EXP2)
            total = jnp.sum(weights, axis=-1, keepdims=True)
            mixed = jnp.dot(weights.astype(BF16), kv[block, 1], preferred_element_type=F32)
            if not first:
                fade = jnp.exp2((old_top - top) * EXP2)
                total += l_s[at, :] * fade
                mixed += acc_s[at, :] * fade
            m_s[at, :] = top
            l_s[at, :] = total
            acc_s[at, :] = mixed
            return carry

        lax.fori_loop(0, (TOK if part is None else HALF) // rows4, chunk, 0, unroll=True)

    attend(gx, True)
    w_up.step(1)
    for s in (1, 2, 3, 4):
        for p in (0, 1):
            arrive("kv", 2 * (s - 1) + p, kv.at[gx_at(-s * d_a), p])
            if s < 4:
                kv_ahead(s + 1, p)
                arrive("kv", 8 + 2 * (s - 1) + p, kv.at[gx_at(s * d_a), p])
                if s < 3:
                    kv_back(s + 1, p)
            if s > 1:
                attend(gx_at((-1 if p == 0 else 1) * (s - 1) * d_a))
        if s > 1:
            w_up.step(s)
        if s == 2:
            local[11].wait()
            w_dn.ahead()
        if s == 4:
            w_dn.step(1)

    theirs, mine = pl.multiple_of((1 - core) * HALF, HALF), pl.multiple_of(core * HALF, HALF)

    def attended(start):
        at = pl.ds(start, HALF)
        return (acc_s[at, :] / l_s[at, :]).astype(BF16)

    last = gx_at(-4 * d_a)
    attend(last, part=1 - core)
    swap_s[0] = attended(theirs)
    push("swap", 0, swap_s.at[0], att.at[gy], {"gy": sib})
    attend(last, part=core)
    att[gy] = attended(mine)
    g_att.start(0)
    for d in range(1, 8):
        arrive("wo", d - 1, wout.at[core, y_at(-d)])
    push("wo", 7, wout.at[core], wout.at[core], {"gy": sib})
    arrive("swap", 0, att.at[sib])
    g_att.start(1)
    w_up.finish()
    push("bulk", 0, wup.at[core], wup.at[core], {"gy": sib})
    local[12].wait()
    w_mg.ahead()
    for s in (1, 2, 3, 4):
        g_att.step(s)
        if s == 1:
            w_dn.step(2)
        if s == 2:
            w_mg.step(1)
        if s == 3:
            w_dn.step(3)
    arrive("wo", 7, wout.at[1 - core])

    total = jnp.zeros((HALF, 2 * HD), F32)
    for j in range(SLOTS):
        total += jnp.dot(att[j], wout[j % 2, j // 2], preferred_element_type=F32)
    for h in (0, 1):
        own = tok[2 * ypos + h, pl.ds(mine, HALF), :].astype(F32)
        aft[2 * ypos + h] = (own + total[:, h * HD : (h + 1) * HD]).astype(BF16)

    g_aft.start(0)
    g_aft.start(1)
    w_mg.step(2)
    for s in (1, 2, 3, 4):
        g_aft.step(s)
        if s == 1:
            w_dn.step(4)
        if s == 2:
            w_mg.step(3)
        if s == 3:
            w_dn.finish()
            push("bulk", 1, wdn.at[core], wdn.at[core], {"gy": sib})
    norm(aft, gsm, xn, HALF, 32)
    arrive("bulk", 0, wup.at[1 - core])

    def mlp_up(r, carry):
        g = r // 2
        at = pl.ds(pl.multiple_of((r % 2) * rows4, rows4), rows4)
        total = jnp.zeros((rows4, FF_DEV), F32)
        for j in range(NZ):
            total += jnp.dot(xn[j, at, :], wup[g, j], preferred_element_type=F32)
        hid[g, at, :] = erf_gelu(total).astype(BF16)
        return carry

    lax.fori_loop(0, 4, mlp_up, 0)
    w_mg.step(4)
    arrive("bulk", 1, wdn.at[1 - core])

    def mlp_down(d):
        dest = y_at(d * d_a)
        part = jnp.zeros((HALF, 2 * HD), F32)
        for g in (0, 1):
            part += lax.dot_general(
                hid[g], wdn[g, dest], (((1,), (1,)), ((), ())), preferred_element_type=F32
            )
        pp[dest, 0] = part[:, :HD].astype(BF16)
        pp[dest, 1] = part[:, HD:].astype(BF16)

    def fold(dest, h, extra):
        pp[dest, h] = (pp[dest, h].astype(F32) + extra.astype(F32)).astype(BF16)

    ahead, behind = {"gy": gy_at(2 * d_a)}, {"gy": gy_at(-2 * d_a)}
    far, near = y_at(4 * d_a), y_at(-3 * d_a)
    mlp_down(4)
    for h in (0, 1):
        push("rs_y", h, pp.at[far, h], ra.at[0, h], ahead)
    mlp_down(-3)
    for h in (0, 1):
        push("rs_y", 8 + h, pp.at[near, h], rb.at[0, h], behind)
    for d in (3, -2, 2, -1, 1, 0):
        mlp_down(d)
    for s in (1, 2, 3):
        to_a, to_b = y_at((4 - s) * d_a), y_at(-(3 - s) * d_a)
        for h in (0, 1):
            arrive("rs_y", 2 * (s - 1) + h, ra.at[s - 1, h])
            fold(to_a, h, ra[s - 1, h])
            push("rs_y", 2 * s + h, pp.at[to_a, h], ra.at[s, h], ahead)
            if s < 3:
                arrive("rs_y", 8 + 2 * (s - 1) + h, rb.at[s - 1, h])
                fold(to_b, h, rb[s - 1, h])
                push("rs_y", 8 + 2 * s + h, pp.at[to_b, h], rb.at[s, h], behind)
    for h in (0, 1):
        arrive("rs_y", 12 + h, rb.at[2, h])
        arrive("rs_y", 6 + h, ra.at[3, h])

    def layer_rows(h):
        mlp_sum = pp[ypos, h].astype(F32) + ra[3, h].astype(F32) + rb[2, h].astype(F32)
        return (aft[2 * ypos + h].astype(F32) + mlp_sum).astype(BF16)

    swap_s[1] = layer_rows(1 - core)
    push("swap", 1, swap_s.at[1], lo_s.at[pl.ds(mine, HALF)], {"gy": sib})
    lo_s[pl.ds(mine, HALF), :] = layer_rows(core)
    w_mg.finish()
    arrive("swap", 1, lo_s.at[pl.ds(theirs, HALF)])
    lo_ref[...] = jnp.transpose(lo_s[...])

    spot = lax.broadcasted_iota(jnp.int32, (GROUPS, TOK), 1).astype(F32)
    eye2 = lax.broadcasted_iota(jnp.int32, (GROUPS, GROUPS), 0) == lax.broadcasted_iota(
        jnp.int32, (GROUPS, GROUPS), 1
    )
    for k in range(4):
        member = jnp.sum(
            jnp.where(eye2, mg_ref[k : k + 1, :].astype(F32), 0.0), axis=1, keepdims=True
        )
        pick = jnp.where(member == spot, 1.0, 0.0).astype(BF16)
        pk[k] = jnp.dot(pick, lo_s[...], preferred_element_type=F32).astype(BF16)

    def merge(j, carry):
        total = jnp.zeros((GROUPS, 2 * HD), F32)
        for k in range(4):
            total += jnp.dot(pk[k], wmg[j, k], preferred_element_type=F32)
        mm[0, j] = total[:, :HD].astype(BF16)
        mm[1, j] = total[:, HD:].astype(BF16)
        return carry

    lax.fori_loop(0, NY, merge, 0)
    push("mg_s", 0, mm.at[1 - core], sm, {"gy": sib})
    arrive("mg_s", 0, sm)
    mm[core] = (mm[core].astype(F32) + sm[...].astype(F32)).astype(BF16)
    for d in (4, 3, 5, 2, 6, 1, 7):
        push("mg_y", d - 1, mm.at[core, y_at(d)], rm.at[d - 1], {"gy": gy_at(2 * d)})
    total = mm[core, ypos].astype(F32)
    for d in range(1, 8):
        arrive("mg_y", d - 1, rm.at[d - 1])
    for d in range(1, 8):
        total += rm[d - 1].astype(F32)
    stk[row] = total.astype(BF16)
    for d in (1, 2, 3):
        push("row", d - 1, stk.at[row], stk.at[row], {"row": row_at(d)})
    wanted = jnp.sum(jnp.where(eye2, src_ref[...].astype(F32), 0.0), axis=1, keepdims=True)
    for d in (1, 2, 3):
        arrive("row", d - 1, stk.at[row_at(-d)])
    place = lax.broadcasted_iota(jnp.int32, (GROUPS, GROUPS), 1).astype(F32)
    total = jnp.zeros((GROUPS, HD), F32)
    for r in range(4):
        pick = jnp.where(wanted == place + float(GROUPS * r), 1.0, 0.0).astype(BF16)
        total += jnp.dot(pick, stk[r], preferred_element_type=F32)
    ret_ref[...] = jnp.transpose(total.astype(BF16))

    for copy in pending:
        copy.wait_send()


def body(
    tokens,
    segments,
    gain_attn,
    w_query,
    w_key,
    w_value,
    w_out,
    gain_mlp,
    w_up,
    w_down,
    w_merge,
    merge_groups,
    sources,
):
    anyspace = pl.BlockSpec(memory_space=pl.ANY)
    vmem = pl.BlockSpec(memory_space=pltpu.VMEM)
    scratch = [
        pltpu.VMEM((SLOTS, TOK, HD), BF16),
        pltpu.VMEM((NZ, TOK, 2 * HD), BF16),
        pltpu.VMEM((NZ, 3, 2 * HD, HD), BF16),
        pltpu.VMEM((TOK, HD), BF16),
        pltpu.VMEM((NZ, 2, TOK, HD), BF16),
        pltpu.VMEM((SLOTS, HALF, HD), BF16),
        pltpu.VMEM((SLOTS, HALF, HD), BF16),
        pltpu.VMEM((NY, HD, 2 * HD), BF16),
        pltpu.VMEM((2, NY, HD, 2 * HD), BF16),
        pltpu.VMEM((2, NZ, 2 * HD, FF_DEV), BF16),
        pltpu.VMEM((2, NZ, 2 * HD, FF_DEV), BF16),
        pltpu.VMEM((NZ, 4, HD, 2 * HD), BF16),
        pltpu.VMEM((2, HALF, FF_DEV), BF16),
        pltpu.VMEM((NY, 2, HALF, HD), BF16),
        pltpu.VMEM((4, 2, HALF, HD), BF16),
        pltpu.VMEM((3, 2, HALF, HD), BF16),
        pltpu.VMEM((TOK, HD), BF16),
        pltpu.VMEM((2, HALF, HD), BF16),
        pltpu.VMEM((4, GROUPS, HD), BF16),
        pltpu.VMEM((2, NY, GROUPS, HD), BF16),
        pltpu.VMEM((NY, GROUPS, HD), BF16),
        pltpu.VMEM((7, GROUPS, HD), BF16),
        pltpu.VMEM((4, GROUPS, HD), BF16),
        pltpu.VMEM((NZ, TOK), jnp.int32),
        pltpu.VMEM((TOK, 1), F32),
        pltpu.VMEM((SLOTS, 1, HD), F32),
        pltpu.VMEM((SLOTS, 1, HD), F32),
        pltpu.VMEM((TOK, 1), F32),
        pltpu.VMEM((TOK, 1), F32),
        pltpu.VMEM((TOK, HD), F32),
        pltpu.VMEM((HD, TOK), BF16),
        pltpu.VMEM((HD, D), BF16),
        pltpu.VMEM((1, NZ * TOK), jnp.int32),
        pltpu.VMEM((4, GROUPS), jnp.int32),
        pltpu.VMEM((1, GROUPS), jnp.int32),
        pltpu.VMEM((1, D), F32),
        pltpu.VMEM((1, D), F32),
        pltpu.SemaphoreType.DMA((LOCAL,)),
    ]
    for count in SEM_COUNTS.values():
        scratch += [pltpu.SemaphoreType.DMA((count,)), pltpu.SemaphoreType.DMA((count,))]
    layer_out, returned = pl.pallas_call(
        kernel,
        out_shape=(
            jax.ShapeDtypeStruct((HD, TOK), BF16),
            jax.ShapeDtypeStruct((HD, GROUPS), BF16),
        ),
        in_specs=[anyspace] * 13,
        out_specs=(vmem, vmem),
        scratch_shapes=scratch,
        compiler_params=pltpu.CompilerParams(
            collective_id=0, has_side_effects=True, vmem_limit_bytes=60 << 20
        ),
        name="layer",
    )(
        tokens[0].T,
        segments,
        gain_attn.reshape(1, D),
        w_query,
        w_key,
        w_value,
        w_out,
        gain_mlp.reshape(1, D),
        w_up,
        w_down.T,
        w_merge,
        merge_groups[0].T,
        sources,
    )
    return (layer_out.T[None], returned.T[None])


def solution(mesh):
    placed = (
        P("row", "gx", "gy"),
        P("row", None),
        P(),
        P("gx", "gy"),
        P("gx", "gy"),
        P("gx", "gy"),
        P("gy", None),
        P(),
        P("gx", "gy"),
        P("gy", "gx"),
        P(None, "gy", "gx"),
        P("row", "gx", None),
        P("row", "gx"),
    )
    return jax.shard_map(
        body,
        mesh=mesh,
        in_specs=placed,
        out_specs=(P("row", "gx", "gy"), P("row", "gx", "gy")),
        check_vma=False,
    )
```

time: 161 us -> 142 us (0.88)
  Pallas kernels: 152 us -> 137 us
  local copies, waits for them, and re-layouts: 7.66 us -> 4.07 us
    pallas_call x1, Pallas kernels: 152 us -> 137 us  [body(): pl.pallas_call(kernel, out_shape=(jax.ShapeDtypeStruct((HD, TOK), BF16),...]
    unnamed x23 -> x6, local copies, waits for them, and re-layouts: 6.2 us -> 2.17 us
where the time goes in v2:
time: 142 us
  Pallas kernels  137 us (96%)
  local copies, waits for them, and re-layouts  4.07 us (3%)
    pallas_call x1, Pallas kernels, body(): pl.pallas_call(kernel, out_shape=(jax.ShapeDtypeStruct((HD, TOK), BF16),...  137 us

profile of v2, /device:TPU:1, one launch (start us, length us, event | category | flops | bytes accessed | tf_op | source)
XLA Modules:
  0.0 141.7 jit_solution(15417476395340195724)
XLA Ops:
  0.6 0.0 copy-start.1
  0.6 1.3 reshape.10.ga_h
  1.9 0.0 copy-done.1
  1.9 0.6 reshape.11.gm_h
  2.5 136.9 %layer.1 = (bf16[104,448]{1,0:T(8,128)(2,1)}, bf16[104,112]{1,0:T(8,128)(2,1)}) custom-call(bf16[104,448]{1,0:T(8,128)(2,1)} %bitcast.15, s32[1,3584]{1,0:T(1,128)} %seg_h.1, f32[1,1664]{1,0:T(1,128)} %reshape.10.ga_h, bf16[208,104]{1,0:T(8,128)(2,1)} %wq_h.1, bf16[208,104]{1,0:T(8,128)(2,1)} %wk_h.1, bf16[208,104]{1,0:T(8,128)(2,1)} %wv_h.1, ...), custom_call_target="tpu_custom_call" | custom-call | tf_op jit(solution)/shard_map/layer/pallas_call | solution.py:632
  139.5 0.0 copy-start
  139.5 1.6 %copy.17 = bf16[1,448,104]{1,2,0:T(8,128)(2,1)} copy(bf16[1,448,104]{1,2,0:T(8,128)(2,1)} %bitcast.14) | data formatting | bytes 186368
  141.0 0.0 copy-done
  141.0 0.6 copy.18
Async XLA Ops:
  0.6 1.3 copy-start.1
  139.5 1.6 %copy-start = (bf16[104,112]{1,0:T(8,128)(2,1)S(1)}, bf16[104,112]{1,0:T(8,128)(2,1)}, u32[]{:S(2)}) copy-start(bf16[104,112]{1,0:T(8,128)(2,1)} %get-tuple-element.5) | copy-start | bytes 69892

commit v3 on v2

--- a/solution.py
+++ b/solution.py
@@ -24,23 +24,25 @@
 EXP2 = HD ** (-0.5) * 1.4426950408889634
 
 HALF = TOK // 2
-
-LOCAL = 13
+PIECE = HALF // 2
+
+LOCAL = 12
 SEM_COUNTS = dict(
     tok_y=14,
-    tok_s=8,
+    tok_s=16,
     kv=14,
     qkv=14,
     wup=7,
+    wupx=3,
     wdn=7,
     wmg=7,
     bulk=2,
     wo=8,
-    swap=2,
+    swap=3,
     att_y=14,
     aft_y=14,
     rs_y=14,
-    mg_s=1,
+    mg_s=8,
     mg_y=7,
     row=3,
 )
@@ -53,12 +55,11 @@
 def kernel(
     tok_h,
     seg_h,
-    ga_h,
+    gain_h,
     wq_h,
     wk_h,
     wv_h,
     wo_h,
-    gm_h,
     wu_h,
     wd_h,
     wm_h,
@@ -101,8 +102,7 @@
     seg_ref,
     mg_ref,
     src_ref,
-    ga_ref,
-    gm_ref,
+    gain_ref,
     loc_sem,
     *sems,
 ):
@@ -155,6 +155,12 @@
             device_id_type=MESH,
         ).wait_recv()
 
+    def quarter(r):
+        return pl.ds(pl.multiple_of(r * (FF_DEV // 4), FF_DEV // 4), FF_DEV // 4)
+
+    def quarter_ref(slot):
+        return wup.at[core, slot, :, quarter(row)]
+
     local = []
     for i, (src, dst) in enumerate(
         (
@@ -166,9 +172,8 @@
             (seg_h, seg_ref),
             (mg_h, mg_ref),
             (src_h, src_ref),
-            (ga_h, ga_ref),
-            (gm_h, gm_ref),
-            (wu_h, wup.at[core, gx]),
+            (gain_h, gain_ref),
+            (wu_h.at[:, quarter(row)], quarter_ref(gx)),
             (wd_h, wdn.at[core, gx]),
             (wm_h, wmg.at[gx]),
         )
@@ -205,20 +210,27 @@
             self.ahead(1, p)
             self.back(1, p)
 
+        def piece(self, s, p):
+            arrive(self.name, 2 * (s - 1) + p, self.part(-s * d_a, p))
+            if s < 4:
+                self.ahead(s + 1, p)
+                arrive(self.name, 8 + 2 * (s - 1) + p, self.part(s * d_a, p))
+                if s < 3:
+                    self.back(s + 1, p)
+
         def step(self, s):
-            for p in (0, 1):
-                arrive(self.name, 2 * (s - 1) + p, self.part(-s * d_a, p))
-                if s < 4:
-                    self.ahead(s + 1, p)
-                    arrive(self.name, 8 + 2 * (s - 1) + p, self.part(s * d_a, p))
-                    if s < 3:
-                        self.back(s + 1, p)
+            self.piece(s, 0)
+            self.piece(s, 1)
 
     def tok_part(k, p):
         return tok.at[gy_at(2 * k), pl.ds(p * HALF, HALF)]
 
-    def across(idx, slot):
-        push("tok_s", idx, tok.at[slot], tok.at[slot], {"gy": sib})
+    def across(idx, k, p):
+        ref = tok_part(k, p)
+        push("tok_s", 2 * idx + p, ref, ref, {"gy": sib})
+
+    def aft_part(k, p):
+        return aft.at[pl.ds(2 * y_at(k), 2), pl.ds(p * PIECE, PIECE)]
 
     def pair_part(buf):
         def part(k, p):
@@ -258,24 +270,55 @@
 
     g_tok = Ring("tok_y", tok_part)
     g_att = Ring("att_y", pair_part(att))
-    g_aft = Ring("aft_y", pair_part(aft))
+    g_aft = Ring("aft_y", aft_part)
     w_qkv = Weights("qkv", wqkv, ((0, 2), (2, 1)))
-    w_up = Weights("wup", wup.at[core], ((0, 208),))
+
+    class Quarters:
+        def ahead(self, s):
+            ref = quarter_ref(gx_at(-(s - 1) * d_a))
+            push("wup", s - 1, ref, ref, {"gx": gx_at(d_a)})
+
+        def back(self, s):
+            ref = quarter_ref(gx_at((s - 1) * d_a))
+            push("wup", 3 + s, ref, ref, {"gx": gx_at(-d_a)})
+
+        def start(self):
+            self.ahead(1)
+            self.back(1)
+
+        def step(self, s):
+            arrive("wup", s - 1, quarter_ref(gx_at(-s * d_a)))
+            if s < 4:
+                self.ahead(s + 1)
+                arrive("wup", 3 + s, quarter_ref(gx_at(s * d_a)))
+                if s < 3:
+                    self.back(s + 1)
+            else:
+                ref = wup.at[core, :, :, quarter(row)]
+                for d in (1, 3, 2):
+                    push("wupx", d - 1, ref, ref, {"row": row_at(d)})
+
+        def finish(self):
+            for d in (1, 2, 3):
+                arrive("wupx", d - 1, wup.at[core, :, :, quarter(row_at(-d))])
+
+    w_up = Quarters()
     w_dn = Weights("wdn", wdn.at[core], ((0, 208),))
     w_mg = Weights("wmg", wmg, ((0, 4),))
 
     g_tok.start(0)
     g_tok.start(1)
-    across(0, gy)
+    across(0, 0, 0)
+    across(0, 0, 1)
     for i in (1, 2, 3):
         local[i].wait()
     w_qkv.ahead()
-    for i in range(4, 10):
+    for i in range(4, 9):
         local[i].wait()
 
     for j in range(SLOTS):
-        gsa[j] = ga_ref[:, j * HD : (j + 1) * HD]
-        gsm[j] = gm_ref[:, j * HD : (j + 1) * HD]
+        gsa[j] = gain_ref[0:1, j * HD : (j + 1) * HD]
+        gsm[j] = gain_ref[1:2, j * HD : (j + 1) * HD]
     for j in range(NY):
         wout_s[j] = wo_ref[:, j * 2 * HD : (j + 1) * 2 * HD]
     for j in range(NZ):
@@ -287,23 +330,20 @@
     qseg[...] = jnp.sum(jnp.where(eye, own_row.astype(F32), 0.0), axis=1, keepdims=True)
 
     for s in (1, 2, 3, 4):
-        g_tok.step(s)
-        across(s, gy_at(-2 * s * d_a))
-        if s < 4:
-            across(4 + s, gy_at(2 * s * d_a))
+        for p in (0, 1):
+            g_tok.piece(s, p)
+            across(s, -s * d_a, p)
+            if s < 4:
+                across(4 + s, s * d_a, p)
         w_qkv.step(s)
-    local[10].wait()
-    w_up.ahead()
-    arrive("tok_s", 0, tok.at[sib])
-    for s in (1, 2, 3, 4):
-        arrive("tok_s", s, tok.at[lax.rem(sib + 2 * s * d_a + 32, 16)])
-        if s < 4:
-            arrive("tok_s", 4 + s, tok.at[lax.rem(sib - 2 * s * d_a + 32, 16)])
-
-    def norm(src, gains, out, count, rows):
+        if s == 2:
+            local[9].wait()
+            w_up.start()
+
+    def norm(src, gains, out, start, count, rows):
 
         def chunk(r, carry):
-            at = pl.ds(pl.multiple_of(r * rows, rows), rows)
+            at = pl.ds(pl.multiple_of(start + r * rows, 16), rows)
             total = src[0, at, :].astype(F32)
             for j in range(1, SLOTS):
                 total += src[j, at, :].astype(F32)
@@ -321,7 +361,19 @@
 
         lax.fori_loop(0, count // rows, chunk, 0)
 
-    norm(tok, gsa, xn, TOK, 64)
+    w_up.step(1)
+
+    def token_slot(slot, p):
+        return tok.at[slot, pl.ds(p * HALF, HALF)]
+
+    for p in (0, 1):
+        arrive("tok_s", p, token_slot(sib, p))
+        for s in (1, 2, 3, 4):
+            arrive("tok_s", 2 * s + p, token_slot(lax.rem(sib + 2 * s * d_a + 32, 16), p))
+            if s < 4:
+                arrive("tok_s", 2 * (4 + s) + p, token_slot(lax.rem(sib - 2 * s * d_a + 32, 16), p))
+        norm(tok, gsa, xn, p * HALF, HALF, PIECE)
+    w_up.step(2)
     w_qkv.finish()
 
     rows2 = TOK // 2
@@ -389,7 +441,7 @@
         lax.fori_loop(0, (TOK if part is None else HALF) // rows4, chunk, 0, unroll=True)
 
     attend(gx, True)
-    w_up.step(1)
+    w_up.step(3)
     for s in (1, 2, 3, 4):
         for p in (0, 1):
             arrive("kv", 2 * (s - 1) + p, kv.at[gx_at(-s * d_a), p])
@@ -400,13 +452,11 @@
                     kv_back(s + 1, p)
             if s > 1:
                 attend(gx_at((-1 if p == 0 else 1) * (s - 1) * d_a))
-        if s > 1:
-            w_up.step(s)
-        if s == 2:
-            local[11].wait()
+        if s == 1:
+            w_up.step(4)
+        if s == 3:
+            local[10].wait()
             w_dn.ahead()
-        if s == 4:
-            w_dn.step(1)
 
     theirs, mine = pl.multiple_of((1 - core) * HALF, HALF), pl.multiple_of(core * HALF, HALF)
 
@@ -426,102 +476,113 @@
     push("wo", 7, wout.at[core], wout.at[core], {"gy": sib})
     arrive("swap", 0, att.at[sib])
     g_att.start(1)
+    w_dn.step(1)
+    for s in (1, 2, 3, 4):
+        g_att.step(s)
+        if s == 2:
+            w_dn.step(2)
+        if s == 3:
+            local[11].wait()
+            w_mg.ahead()
+    arrive("wo", 7, wout.at[1 - core])
     w_up.finish()
     push("bulk", 0, wup.at[core], wup.at[core], {"gy": sib})
-    local[12].wait()
-    w_mg.ahead()
-    for s in (1, 2, 3, 4):
-        g_att.step(s)
-        if s == 1:
-            w_dn.step(2)
-        if s == 2:
-            w_mg.step(1)
-        if s == 3:
-            w_dn.step(3)
-    arrive("wo", 7, wout.at[1 - core])
-
-    total = jnp.zeros((HALF, 2 * HD), F32)
-    for j in range(SLOTS):
-        total += jnp.dot(att[j], wout[j % 2, j // 2], preferred_element_type=F32)
-    for h in (0, 1):
-        own = tok[2 * ypos + h, pl.ds(mine, HALF), :].astype(F32)
-        aft[2 * ypos + h] = (own + total[:, h * HD : (h + 1) * HD]).astype(BF16)
-
-    g_aft.start(0)
-    g_aft.start(1)
-    w_mg.step(2)
-    for s in (1, 2, 3, 4):
+
+    for p in (0, 1):
+        at = pl.ds(p * PIECE, PIECE)
+        total = jnp.zeros((PIECE, 2 * HD), F32)
+        for j in range(SLOTS):
+            total += jnp.dot(att[j, at, :], wout[j % 2, j // 2], preferred_element_type=F32)
+        for h in (0, 1):
+            own = tok[2 * ypos + h, pl.ds(pl.multiple_of(mine + p * PIECE, 16), PIECE), :].astype(F32)
+            aft[2 * ypos + h, at, :] = (own + total[:, h * HD : (h + 1) * HD]).astype(BF16)
+        g_aft.start(p)
+    w_dn.step(3)
+    for s in (1, 2, 3):
         g_aft.step(s)
         if s == 1:
+            w_mg.step(1)
+        if s == 2:
             w_dn.step(4)
-        if s == 2:
-            w_mg.step(3)
         if s == 3:
+            w_mg.step(2)
             w_dn.finish()
             push("bulk", 1, wdn.at[core], wdn.at[core], {"gy": sib})
-    norm(aft, gsm, xn, HALF, 32)
     arrive("bulk", 0, wup.at[1 - core])
 
-    def mlp_up(r, carry):
-        g = r // 2
-        at = pl.ds(pl.multiple_of((r % 2) * rows4, rows4), rows4)
-        total = jnp.zeros((rows4, FF_DEV), F32)
-        for j in range(NZ):
-            total += jnp.dot(xn[j, at, :], wup[g, j], preferred_element_type=F32)
-        hid[g, at, :] = erf_gelu(total).astype(BF16)
-        return carry
-
-    lax.fori_loop(0, 4, mlp_up, 0)
-    w_mg.step(4)
-    arrive("bulk", 1, wdn.at[1 - core])
-
-    def mlp_down(d):
+    def mlp_up(p):
+        at = pl.ds(p * PIECE, PIECE)
+
+        def units(g, carry):
+            total = jnp.zeros((PIECE, FF_DEV), F32)
+            for j in range(NZ):
+                total += jnp.dot(xn[j, at, :], wup[g, j], preferred_element_type=F32)
+            hid[g, at, :] = erf_gelu(total).astype(BF16)
+            return carry
+
+        lax.fori_loop(0, 2, units, 0)
+
+    def mlp_down(d, p):
         dest = y_at(d * d_a)
-        part = jnp.zeros((HALF, 2 * HD), F32)
+        part = jnp.zeros((PIECE, 2 * HD), F32)
         for g in (0, 1):
             part += lax.dot_general(
-                hid[g], wdn[g, dest], (((1,), (1,)), ((), ())), preferred_element_type=F32
+                hid[g, pl.ds(p * PIECE, PIECE), :],
+                wdn[g, dest],
+                (((1,), (1,)), ((), ())),
+                preferred_element_type=F32,
             )
-        pp[dest, 0] = part[:, :HD].astype(BF16)
-        pp[dest, 1] = part[:, HD:].astype(BF16)
-
-    def fold(dest, h, extra):
-        pp[dest, h] = (pp[dest, h].astype(F32) + extra.astype(F32)).astype(BF16)
+        pp[dest, p, 0] = part[:, :HD].astype(BF16)
+        pp[dest, p, 1] = part[:, HD:].astype(BF16)
+
+    def fold(dest, p, extra):
+        pp[dest, p] = (pp[dest, p].astype(F32) + extra.astype(F32)).astype(BF16)
 
     ahead, behind = {"gy": gy_at(2 * d_a)}, {"gy": gy_at(-2 * d_a)}
     far, near = y_at(4 * d_a), y_at(-3 * d_a)
-    mlp_down(4)
-    for h in (0, 1):
-        push("rs_y", h, pp.at[far, h], ra.at[0, h], ahead)
-    mlp_down(-3)
-    for h in (0, 1):
-        push("rs_y", 8 + h, pp.at[near, h], rb.at[0, h], behind)
+    for p in (0, 1):
+        g_aft.piece(4, p)
+        norm(aft, gsm, xn, p * PIECE, PIECE, PIECE)
+        mlp_up(p)
+        if p == 0:
+            arrive("bulk", 1, wdn.at[1 - core])
+        mlp_down(4, p)
+        push("rs_y", p, pp.at[far, p], ra.at[0, p], ahead)
+        mlp_down(-3, p)
+        push("rs_y", 8 + p, pp.at[near, p], rb.at[0, p], behind)
+    w_mg.step(3)
     for d in (3, -2, 2, -1, 1, 0):
-        mlp_down(d)
+        for p in (0, 1):
+            mlp_down(d, p)
     for s in (1, 2, 3):
         to_a, to_b = y_at((4 - s) * d_a), y_at(-(3 - s) * d_a)
-        for h in (0, 1):
-            arrive("rs_y", 2 * (s - 1) + h, ra.at[s - 1, h])
-            fold(to_a, h, ra[s - 1, h])
-            push("rs_y", 2 * s + h, pp.at[to_a, h], ra.at[s, h], ahead)
+        for p in (0, 1):
+            arrive("rs_y", 2 * (s - 1) + p, ra.at[s - 1, p])
+            fold(to_a, p, ra[s - 1, p])
+            push("rs_y", 2 * s + p, pp.at[to_a, p], ra.at[s, p], ahead)
             if s < 3:
-                arrive("rs_y", 8 + 2 * (s - 1) + h, rb.at[s - 1, h])
-                fold(to_b, h, rb[s - 1, h])
-                push("rs_y", 8 + 2 * s + h, pp.at[to_b, h], rb.at[s, h], behind)
-    for h in (0, 1):
-        arrive("rs_y", 12 + h, rb.at[2, h])
-        arrive("rs_y", 6 + h, ra.at[3, h])
-
-    def layer_rows(h):
-        mlp_sum = pp[ypos, h].astype(F32) + ra[3, h].astype(F32) + rb[2, h].astype(F32)
-        return (aft[2 * ypos + h].astype(F32) + mlp_sum).astype(BF16)
-
-    swap_s[1] = layer_rows(1 - core)
-    push("swap", 1, swap_s.at[1], lo_s.at[pl.ds(mine, HALF)], {"gy": sib})
-    lo_s[pl.ds(mine, HALF), :] = layer_rows(core)
+                arrive("rs_y", 8 + 2 * (s - 1) + p, rb.at[s - 1, p])
+                fold(to_b, p, rb[s - 1, p])
+                push("rs_y", 8 + 2 * s + p, pp.at[to_b, p], rb.at[s, p], behind)
+        if s == 1:
+            w_mg.step(4)
+
+    def layer_rows(p, h):
+        mlp_sum = pp[ypos, p, h].astype(F32) + ra[3, p, h].astype(F32) + rb[2, p, h].astype(F32)
+        return (aft[2 * ypos + h, pl.ds(p * PIECE, PIECE), :].astype(F32) + mlp_sum).astype(BF16)
+
+    def rows_at(start, p):
+        return pl.ds(pl.multiple_of(start + p * PIECE, 16), PIECE)
+
+    for p in (0, 1):
+        arrive("rs_y", 12 + p, rb.at[2, p])
+        arrive("rs_y", 6 + p, ra.at[3, p])
+        swap_s[1, pl.ds(p * PIECE, PIECE), :] = layer_rows(p, 1 - core)
+        push("swap", 1 + p, swap_s.at[1, pl.ds(p * PIECE, PIECE)], lo_s.at[rows_at(mine, p)], {"gy": sib})
+        lo_s[rows_at(mine, p), :] = layer_rows(p, core)
     w_mg.finish()
-    arrive("swap", 1, lo_s.at[pl.ds(theirs, HALF)])
-    lo_ref[...] = jnp.transpose(lo_s[...])
+    for p in (0, 1):
+        arrive("swap", 1 + p, lo_s.at[rows_at(theirs, p)])
 
     spot = lax.broadcasted_iota(jnp.int32, (GROUPS, TOK), 1).astype(F32)
     eye2 = lax.broadcasted_iota(jnp.int32, (GROUPS, GROUPS), 0) == lax.broadcasted_iota(
@@ -534,20 +595,22 @@
         pick = jnp.where(member == spot, 1.0, 0.0).astype(BF16)
         pk[k] = jnp.dot(pick, lo_s[...], preferred_element_type=F32).astype(BF16)
 
-    def merge(j, carry):
+    others = (4, 3, 5, 2, 6, 1, 7, 0)
+    for i, d in enumerate(others):
+        dest = y_at(d)
         total = jnp.zeros((GROUPS, 2 * HD), F32)
         for k in range(4):
-            total += jnp.dot(pk[k], wmg[j, k], preferred_element_type=F32)
-        mm[0, j] = total[:, :HD].astype(BF16)
-        mm[1, j] = total[:, HD:].astype(BF16)
-        return carry
-
-    lax.fori_loop(0, NY, merge, 0)
-    push("mg_s", 0, mm.at[1 - core], sm, {"gy": sib})
-    arrive("mg_s", 0, sm)
-    mm[core] = (mm[core].astype(F32) + sm[...].astype(F32)).astype(BF16)
-    for d in (4, 3, 5, 2, 6, 1, 7):
-        push("mg_y", d - 1, mm.at[core, y_at(d)], rm.at[d - 1], {"gy": gy_at(2 * d)})
+            total += jnp.dot(pk[k], wmg[dest, k], preferred_element_type=F32)
+        mm[0, dest] = total[:, :HD].astype(BF16)
+        mm[1, dest] = total[:, HD:].astype(BF16)
+        push("mg_s", i, mm.at[1 - core, dest], sm.at[dest], {"gy": sib})
+    for i, d in enumerate(others):
+        dest = y_at(d)
+        arrive("mg_s", i, sm.at[dest])
+        mm[core, dest] = (mm[core, dest].astype(F32) + sm[dest].astype(F32)).astype(BF16)
+        if d:
+            push("mg_y", d - 1, mm.at[core, dest], rm.at[d - 1], {"gy": gy_at(2 * d)})
+    lo_ref[...] = jnp.transpose(lo_s[...])
     total = mm[core, ypos].astype(F32)
     for d in range(1, 8):
         arrive("mg_y", d - 1, rm.at[d - 1])
@@ -601,9 +664,9 @@
         pltpu.VMEM((2, NZ, 2 * HD, FF_DEV), BF16),
         pltpu.VMEM((NZ, 4, HD, 2 * HD), BF16),
         pltpu.VMEM((2, HALF, FF_DEV), BF16),
-        pltpu.VMEM((NY, 2, HALF, HD), BF16),
-        pltpu.VMEM((4, 2, HALF, HD), BF16),
-        pltpu.VMEM((3, 2, HALF, HD), BF16),
+        pltpu.VMEM((NY, 2, 2, PIECE, HD), BF16),
+        pltpu.VMEM((4, 2, 2, PIECE, HD), BF16),
+        pltpu.VMEM((3, 2, 2, PIECE, HD), BF16),
         pltpu.VMEM((TOK, HD), BF16),
         pltpu.VMEM((2, HALF, HD), BF16),
         pltpu.VMEM((4, GROUPS, HD), BF16),
@@ -623,8 +686,7 @@
         pltpu.VMEM((1, NZ * TOK), jnp.int32),
         pltpu.VMEM((4, GROUPS), jnp.int32),
         pltpu.VMEM((1, GROUPS), jnp.int32),
-        pltpu.VMEM((1, D), F32),
-        pltpu.VMEM((1, D), F32),
+        pltpu.VMEM((2, D), F32),
         pltpu.SemaphoreType.DMA((LOCAL,)),
     ]
     for count in SEM_COUNTS.values():
@@ -635,7 +697,7 @@
             jax.ShapeDtypeStruct((HD, TOK), BF16),
             jax.ShapeDtypeStruct((HD, GROUPS), BF16),
         ),
-        in_specs=[anyspace] * 13,
+        in_specs=[anyspace] * 12,
         out_specs=(vmem, vmem),
         scratch_shapes=scratch,
         compiler_params=pltpu.CompilerParams(
@@ -645,12 +707,11 @@
     )(
         tokens[0].T,
         segments,
-        gain_attn.reshape(1, D),
+        jnp.stack([gain_attn, gain_mlp]),
         w_query,
         w_key,
         w_value,
         w_out,
-        gain_mlp.reshape(1, D),
         w_up,
         w_down.T,
         w_merge,

time: 142 us -> 135 us (0.951)
  Pallas kernels: 137 us -> 131 us
    pallas_call x1, Pallas kernels: 137 us -> 131 us  [body(): pl.pallas_call(kernel, out_shape=(jax.ShapeDtypeStruct((HD, TOK), BF16),...]
    reshape x2 -> x0, local copies, waits for them, and re-layouts: 1.9 us -> none  [the longest x1 1.3 us: body(): gain_attn.reshape(1, D)]
where the time goes in v3:
time: 135 us
  Pallas kernels  131 us (97%)
  local copies, waits for them, and re-layouts  2.88 us (2%)
    pallas_call x1, Pallas kernels, body(): pl.pallas_call(kernel, out_shape=(jax.ShapeDtypeStruct((HD, TOK), BF16),...  131 us

profile of v3, /device:TPU:1, one launch (start us, length us, event | category | flops | bytes accessed | tf_op | source)
XLA Modules:
  0.0 135.1 jit_solution(9620319425853852402)
XLA Ops:
  0.6 0.0 copy-start.1
  0.6 0.7 stack.9
  1.3 0.0 copy-done.1
  1.4 0.6 pad_maximum_fusion.gain_h
  2.0 130.9 %layer.1 = (bf16[104,448]{1,0:T(8,128)(2,1)}, bf16[104,112]{1,0:T(8,128)(2,1)}) custom-call(bf16[104,448]{1,0:T(8,128)(2,1)} %bitcast.15, s32[1,3584]{1,0:T(1,128)} %seg_h.1, f32[2,1664]{1,0:T(2,128)} %pad_maximum_fusion.gain_h, bf16[208,104]{1,0:T(8,128)(2,1)} %wq_h.1, bf16[208,104]{1,0:T(8,128)(2,1)} %wk_h.1, bf16[208,104]{1,0:T(8,128)(2,1)} %wv_h.1, ...), custom_call_target="tpu_custom_call" | custom-call | tf_op jit(solution)/shard_map/layer/pallas_call | solution.py:694
  132.9 0.0 copy-start
  132.9 1.6 %copy.17 = bf16[1,448,104]{1,2,0:T(8,128)(2,1)} copy(bf16[1,448,104]{1,2,0:T(8,128)(2,1)} %bitcast.14) | data formatting | bytes 186368
  134.5 0.0 copy-done
  134.5 0.6 copy.18
  (1 shorter events, 0.0 us)
Async XLA Ops:
  0.6 0.7 copy-start.1
  132.9 1.6 %copy-start = (bf16[104,112]{1,0:T(8,128)(2,1)S(1)}, bf16[104,112]{1,0:T(8,128)(2,1)}, u32[]{:S(2)}) copy-start(bf16[104,112]{1,0:T(8,128)(2,1)} %get-tuple-element.5) | copy-start | bytes 69892

commit v4 on v3

--- a/solution.py
+++ b/solution.py
@@ -219,8 +219,15 @@
                     self.back(s + 1, p)
 
         def step(self, s):
-            self.piece(s, 0)
-            self.piece(s, 1)
+            for p in (0, 1):
+                arrive(self.name, 2 * (s - 1) + p, self.part(-s * d_a, p))
+                if s < 4:
+                    self.ahead(s + 1, p)
+            for p in (0, 1):
+                if s < 4:
+                    arrive(self.name, 8 + 2 * (s - 1) + p, self.part(s * d_a, p))
+                    if s < 3:
+                        self.back(s + 1, p)
 
     def tok_part(k, p):
         return tok.at[gy_at(2 * k), pl.ds(p * HALF, HALF)]
@@ -318,16 +325,6 @@
 
     for j in range(SLOTS):
         gsa[j] = gain_ref[0:1, j * HD : (j + 1) * HD]
-        gsm[j] = gain_ref[1:2, j * HD : (j + 1) * HD]
-    for j in range(NY):
-        wout_s[j] = wo_ref[:, j * 2 * HD : (j + 1) * 2 * HD]
-    for j in range(NZ):
-        seg8[j : j + 1, :] = seg_ref[:, j * TOK : (j + 1) * TOK]
-    own_row = seg8[pl.ds(gx, 1), :]
-    eye = lax.broadcasted_iota(jnp.int32, (TOK, TOK), 0) == lax.broadcasted_iota(
-        jnp.int32, (TOK, TOK), 1
-    )
-    qseg[...] = jnp.sum(jnp.where(eye, own_row.astype(F32), 0.0), axis=1, keepdims=True)
 
     for s in (1, 2, 3, 4):
         for p in (0, 1):
@@ -373,7 +370,6 @@
             if s < 4:
                 arrive("tok_s", 2 * (4 + s) + p, token_slot(lax.rem(sib - 2 * s * d_a + 32, 16), p))
         norm(tok, gsa, xn, p * HALF, HALF, PIECE)
-    w_up.step(2)
     w_qkv.finish()
 
     rows2 = TOK // 2
@@ -405,6 +401,8 @@
         kv_ahead(1, p)
         kv_back(1, p)
     project(0)
+    for j in range(NY):
+        wout_s[j] = wo_ref[:, j * 2 * HD : (j + 1) * 2 * HD]
     for d in range(1, 8):
         to = y_at(d)
         push("wo", d - 1, wout_s.at[to], wout.at[core, ypos], {"gy": gy_at(2 * d)})
@@ -440,8 +438,17 @@
 
         lax.fori_loop(0, (TOK if part is None else HALF) // rows4, chunk, 0, unroll=True)
 
+    for j in range(NZ):
+        seg8[j : j + 1, :] = seg_ref[:, j * TOK : (j + 1) * TOK]
+    own_row = seg8[pl.ds(gx, 1), :]
+    eye = lax.broadcasted_iota(jnp.int32, (TOK, TOK), 0) == lax.broadcasted_iota(
+        jnp.int32, (TOK, TOK), 1
+    )
+    qseg[...] = jnp.sum(jnp.where(eye, own_row.astype(F32), 0.0), axis=1, keepdims=True)
+    for j in range(SLOTS):
+        gsm[j] = gain_ref[1:2, j * HD : (j + 1) * HD]
     attend(gx, True)
-    w_up.step(3)
+    w_up.step(2)
     for s in (1, 2, 3, 4):
         for p in (0, 1):
             arrive("kv", 2 * (s - 1) + p, kv.at[gx_at(-s * d_a), p])
@@ -452,9 +459,9 @@
                     kv_back(s + 1, p)
             if s > 1:
                 attend(gx_at((-1 if p == 0 else 1) * (s - 1) * d_a))
-        if s == 1:
-            w_up.step(4)
-        if s == 3:
+        if s < 3:
+            w_up.step(s + 2)
+        if s == 4:
             local[10].wait()
             w_dn.ahead()
 
@@ -560,6 +567,7 @@
             arrive("rs_y", 2 * (s - 1) + p, ra.at[s - 1, p])
             fold(to_a, p, ra[s - 1, p])
             push("rs_y", 2 * s + p, pp.at[to_a, p], ra.at[s, p], ahead)
+        for p in (0, 1):
             if s < 3:
                 arrive("rs_y", 8 + 2 * (s - 1) + p, rb.at[s - 1, p])
                 fold(to_b, p, rb[s - 1, p])

time: 135 us -> 134 us (level)
  no operation moved by 1% of the time
where the time goes in v4:
time: 134 us
  Pallas kernels  130 us (97%)
  local copies, waits for them, and re-layouts  2.88 us (2%)
    pallas_call x1, Pallas kernels, body(): pl.pallas_call(kernel, out_shape=(jax.ShapeDtypeStruct((HD, TOK), BF16),...  130 us

profile of v4, /device:TPU:1, one launch (start us, length us, event | category | flops | bytes accessed | tf_op | source)
XLA Modules:
  0.0 134.0 jit_solution(5685212504998728838)
XLA Ops:
  0.6 0.0 copy-start.1
  0.6 0.7 stack.9
  1.3 0.0 copy-done.1
  1.4 0.6 pad_maximum_fusion.gain_h
  2.0 129.9 %layer.1 = (bf16[104,448]{1,0:T(8,128)(2,1)}, bf16[104,112]{1,0:T(8,128)(2,1)}) custom-call(bf16[104,448]{1,0:T(8,128)(2,1)} %bitcast.15, s32[1,3584]{1,0:T(1,128)} %seg_h.1, f32[2,1664]{1,0:T(2,128)} %pad_maximum_fusion.gain_h, bf16[208,104]{1,0:T(8,128)(2,1)} %wq_h.1, bf16[208,104]{1,0:T(8,128)(2,1)} %wk_h.1, bf16[208,104]{1,0:T(8,128)(2,1)} %wv_h.1, ...), custom_call_target="tpu_custom_call" | custom-call | tf_op jit(solution)/shard_map/layer/pallas_call | solution.py:702
  131.9 0.0 copy-start
  131.9 1.6 %copy.17 = bf16[1,448,104]{1,2,0:T(8,128)(2,1)} copy(bf16[1,448,104]{1,2,0:T(8,128)(2,1)} %bitcast.14) | data formatting | bytes 186368
  133.4 0.0 copy-done
  133.4 0.6 copy.18
  (1 shorter events, 0.0 us)
Async XLA Ops:
  0.6 0.7 copy-start.1
  131.9 1.6 %copy-start = (bf16[104,112]{1,0:T(8,128)(2,1)S(1)}, bf16[104,112]{1,0:T(8,128)(2,1)}, u32[]{:S(2)}) copy-start(bf16[104,112]{1,0:T(8,128)(2,1)} %get-tuple-element.5) | copy-start | bytes 69892
